TPU v7x, 32 devices: a whole 2x2x4 slice. The times are simulated.
32 devices in a mesh: section: 4 (over y, x), dp: 8 (over z, core).
Axes of the slice: x: 2, y: 2, z: 4, core: 2. Of those that a mesh axis runs over, the one named last changes fastest.
Arguments:
- block_input: bfloat16 [48, 202, 768], P('dp'), may hold values from -6 to 6
- cotangent: bfloat16 [48, 202, 768], P('dp'), may hold values from -6 to 6
- lengths: int32 [48], P('dp'), may hold values from 1 to 202, 4848 in all
- predicted: int32 [48, 202], P('dp'), may hold values from 0 to 1, as said below
- slab: bfloat16 [4, 768, 4608], P('section')
- in_bias: float32 [4, 3072], P('section'), may hold values from -1.2 to 1.2
- norm_gain: float32 [4, 768], P('section'), may hold values from 0.5 to 1.5
- norm_bias: float32 [4, 768], P('section'), may hold values from -1.8 to 1.8
- feature_draws: int32 [12, 64, 32], replicated, may hold values from -4 to 4
Outputs:
- section_out: bfloat16 [4, 48, 202, 768], P('section', 'dp')
- section_grad: bfloat16 [4, 48, 202, 768], P('section', 'dp')
- slab_grad: float32 [4, 768, 4608], P('section', 'dp')
- bias_grad: float32 [4, 3072], P('section', 'dp')
- gain_grad: float32 [4, 768], P('section', 'dp')
- shift_grad: float32 [4, 768], P('section', 'dp')
Inputs may be any that keep to these rules, and one draw needn't show every extreme that they name: `lengths`: a molecule's tokens fill its first positions; padding positions are never read as keys. `predicted`: 1 marks a masked-prediction position; marks at padding positions count for nothing; some molecules have none.
All inputs are finite; a program needn't handle non-finite values. No bound on the sum of `lengths` on one device may be relied on, other than what follows from the above.
Results may differ from a plain program's by a relative error of at most 0.01.
Values may be sent and summed in bfloat16 or wider, within the bound.
A program may use at most 192 MiB of HBM per device.

v0:
```python
import jax
import jax.numpy as jnp
from jax import lax
from jax.sharding import PartitionSpec as P

MB_MOL = 1


highest = lax.Precision.HIGHEST
norm_epsilon = 1e-05


def shifted(array, axis, by):
    length = lax.axis_size(axis)
    pairs = [(i, i + by) for i in range(length) if 0 <= i + by < length]
    return lax.ppermute(array, axis, pairs)


def layer_norm(residual_sum, scale_row, shift_row):
    centered = residual_sum - jnp.mean(residual_sum, axis=-1, keepdims=True)
    variance = jnp.mean(centered * centered, axis=-1, keepdims=True)
    return centered * lax.rsqrt(variance + norm_epsilon) * scale_row + shift_row


def linear_mix(projected, valid_mask, feature_map):
    head_count, head_dim = (feature_map.shape[0], feature_map.shape[1])
    model_width = projected.shape[-1] // 3
    split_shape = projected.shape[:2] + (head_count, head_dim)
    queries = projected[..., :model_width].reshape(split_shape)
    keys_part = projected[..., model_width : 2 * model_width].reshape(split_shape)
    values_part = projected[..., 2 * model_width :].reshape(split_shape)
    query_feat = jax.nn.softplus(
        jnp.einsum("mlhd,hdf->mlhf", queries, feature_map, precision=highest)
    )
    key_feat = jax.nn.softplus(
        jnp.einsum("mlhd,hdf->mlhf", keys_part, feature_map, precision=highest)
    )
    key_feat = key_feat * valid_mask[:, :, None, None]
    summary = jnp.einsum("mlhf,mlhd->mhfd", key_feat, values_part, precision=highest)
    totals = jnp.sum(key_feat, axis=1)
    numerator = jnp.einsum("mlhf,mhfd->mlhd", query_feat, summary, precision=highest)
    denominator = jnp.einsum("mlhf,mhf->mlh", query_feat, totals, precision=highest)
    return (numerator / denominator[..., None]).reshape(projected.shape[:2] + (model_width,))


def contract_rows(left, right):
    return lax.dot_general(
        left, right, (((0,), (0,)), ((), ())), preferred_element_type=jnp.float32
    )


def contract_cols(left, right):
    return lax.dot_general(
        left, right, (((1,), (1,)), ((), ())), preferred_element_type=jnp.float32
    )


def store_slot(buffer, value, micro_slot, active):
    previous = lax.dynamic_index_in_dim(buffer, micro_slot, 0, keepdims=False)
    return lax.dynamic_update_index_in_dim(
        buffer, jnp.where(active, value, previous), micro_slot, 0
    )


def shards(
    block_input, cotangent, lengths, predicted, slab, in_bias, norm_gain, norm_bias, feature_draws
):
    section_index = lax.axis_index("section")
    section_count = lax.axis_size("section")
    is_attention = section_index % 2 == 0
    molecules, length, model_width = block_input.shape
    micro_count = molecules // MB_MOL
    row_count = MB_MOL * length
    hidden_width = in_bias.shape[1]
    weight = slab[0]
    bias_row = in_bias[0]
    scale_row = norm_gain[0]
    shift_row = norm_bias[0]
    head_dim = feature_draws.shape[1]
    feature_map = feature_draws.astype(jnp.float32) * jnp.sqrt(3.0 / (20.0 * head_dim))
    received = shifted(weight[:, 4 * model_width :], "section", 1)
    down_full = jnp.concatenate([received, weight[:, 4 * model_width :]], axis=1)
    positions = lax.broadcasted_iota(jnp.int32, (molecules, length), 1)
    valid_all = (positions < lengths[:, None]).astype(jnp.float32)
    target_mask = (valid_all * predicted.astype(jnp.float32)).astype(jnp.bfloat16)
    targets = cotangent * target_mask[:, :, None]
    valid_micro = valid_all.reshape(micro_count, MB_MOL, length)

    def attend_forward(current, valid_mask):
        projected = (
            jnp.dot(current, weight[:, : 3 * model_width], preferred_element_type=jnp.float32)
            + bias_row[: 3 * model_width]
        )
        mixed_heads = linear_mix(
            projected.reshape(MB_MOL, length, 3 * model_width), valid_mask, feature_map
        )
        mixed_heads = mixed_heads.reshape(row_count, model_width)
        branch = (
            contract_cols(
                mixed_heads.astype(jnp.bfloat16), weight[:, 3 * model_width : 4 * model_width]
            )
            + bias_row[3 * model_width :]
        )
        residual_sum = current.astype(jnp.float32) + branch
        normed = layer_norm(residual_sum, scale_row, shift_row).astype(jnp.bfloat16)
        return (normed, jnp.concatenate([projected, mixed_heads], axis=1), residual_sum)

    def feed_forward(current, valid_mask):
        hidden_pre = (
            jnp.dot(current, weight[:, :hidden_width], preferred_element_type=jnp.float32)
            + bias_row
        )
        hidden = jax.nn.gelu(hidden_pre, approximate=False).astype(jnp.bfloat16)
        branch = contract_cols(hidden, down_full)
        residual_sum = current.astype(jnp.float32) + branch
        normed = layer_norm(residual_sum, scale_row, shift_row).astype(jnp.bfloat16)
        return (normed, hidden_pre, residual_sum)

    def sublayer_forward(current, valid_mask):
        return lax.cond(is_attention, attend_forward, feed_forward, current, valid_mask)

    def norm_backward(residual_sum, grad_output):
        _, pullback = jax.vjp(layer_norm, residual_sum, scale_row, shift_row)
        return pullback(grad_output.astype(jnp.float32))

    def attend_backward(current, grad_output, kept_state, residual_sum, valid_mask):
        back_residual, back_scale, back_shift = norm_backward(residual_sum, grad_output)
        back_branch = back_residual.astype(jnp.bfloat16)
        projected = kept_state[:, : 3 * model_width]
        mixed_low = kept_state[:, 3 * model_width :].astype(jnp.bfloat16)
        back_out_weight = contract_rows(back_branch, mixed_low)
        back_mixed = jnp.dot(
            back_branch,
            weight[:, 3 * model_width : 4 * model_width],
            preferred_element_type=jnp.float32,
        )
        _, pullback = jax.vjp(
            lambda value: linear_mix(value, valid_mask, feature_map),
            projected.reshape(MB_MOL, length, 3 * model_width),
        )
        back_projected = pullback(back_mixed.reshape(MB_MOL, length, model_width))[0]
        back_projected = back_projected.reshape(row_count, 3 * model_width).astype(jnp.bfloat16)
        back_in_weight = contract_rows(current, back_projected)
        back_current = back_residual + contract_cols(back_projected, weight[:, : 3 * model_width])
        spare_zeros = jnp.zeros((model_width, 2 * model_width), jnp.float32)
        own_grads = jnp.concatenate([back_in_weight, back_out_weight, spare_zeros], axis=1)
        bias_grads = jnp.concatenate(
            [
                jnp.sum(back_projected.astype(jnp.float32), axis=0),
                jnp.sum(back_branch.astype(jnp.float32), axis=0),
            ]
        )
        return (
            back_current.astype(jnp.bfloat16),
            own_grads,
            spare_zeros,
            bias_grads,
            back_scale,
            back_shift,
        )

    def feed_backward(current, grad_output, hidden_pre, residual_sum, valid_mask):
        back_residual, back_scale, back_shift = norm_backward(residual_sum, grad_output)
        back_branch = back_residual.astype(jnp.bfloat16)
        hidden = jax.nn.gelu(hidden_pre, approximate=False).astype(jnp.bfloat16)
        back_down = contract_rows(back_branch, hidden)
        back_hidden = jnp.dot(back_branch, down_full, preferred_element_type=jnp.float32)
        _, pullback = jax.vjp(lambda value: jax.nn.gelu(value, approximate=False), hidden_pre)
        back_pre = pullback(back_hidden)[0].astype(jnp.bfloat16)
        back_up = contract_rows(current, back_pre)
        back_current = back_residual + contract_cols(back_pre, weight[:, :hidden_width])
        own_grads = jnp.concatenate([back_up, back_down[:, 2 * model_width :]], axis=1)
        bias_grads = jnp.sum(back_pre.astype(jnp.float32), axis=0)
        return (
            back_current.astype(jnp.bfloat16),
            own_grads,
            back_down[:, : 2 * model_width],
            bias_grads,
            back_scale,
            back_shift,
        )

    def sublayer_backward(current, grad_output, kept_state, residual_sum, valid_mask):
        return lax.cond(
            is_attention,
            attend_backward,
            feed_backward,
            current,
            grad_output,
            kept_state,
            residual_sum,
            valid_mask,
        )

    def forward_round(state, round_index, incoming):
        micro_index = round_index - section_index
        active = (micro_index >= 0) & (micro_index < micro_count)
        micro_slot = jnp.clip(micro_index, 0, micro_count - 1)
        own_input = lax.dynamic_index_in_dim(block_input, micro_slot, 0, keepdims=False)
        current = jnp.where(section_index == 0, own_input, incoming)
        valid_mask = lax.dynamic_index_in_dim(valid_micro, micro_slot, 0, keepdims=False)

        def resting(current_arg, valid_arg):
            return (
                jnp.zeros((row_count, model_width), jnp.bfloat16),
                jnp.zeros((row_count, hidden_width), jnp.float32),
                jnp.zeros((row_count, model_width), jnp.float32),
            )

        normed, kept_state, residual_sum = lax.cond(
            active, sublayer_forward, resting, current, valid_mask
        )
        new_state = [
            store_slot(state[0], normed, micro_slot, active),
            store_slot(state[1], current, micro_slot, active),
        ]
        return (tuple(new_state), normed)

    state = [
        jnp.zeros((micro_count, row_count, model_width), jnp.bfloat16),
        jnp.zeros((micro_count, row_count, model_width), jnp.bfloat16),
    ]
    state = tuple(state)
    round_count = micro_count + section_count - 1

    def forward_scan(carry, round_index):
        state_now, incoming = carry
        state_now, normed = forward_round(state_now, round_index, incoming)
        incoming = shifted(normed, "section", 1)
        return ((state_now, incoming), None)

    empty_rows = jnp.zeros((row_count, model_width), jnp.bfloat16)
    (state, incoming), _ = lax.scan(forward_scan, (state, empty_rows), jnp.arange(round_count - 1))
    state, _ = forward_round(state, round_count - 1, incoming)

    def backward_round(carry, round_index, incoming):
        totals, grads_buffer = carry
        micro_index = round_index - (section_count - 1 - section_index)
        active = (micro_index >= 0) & (micro_index < micro_count)
        micro_slot = jnp.clip(micro_index, 0, micro_count - 1)
        own_target = lax.dynamic_index_in_dim(targets, micro_slot, 0, keepdims=False)
        grad_output = jnp.where(section_index == section_count - 1, own_target, incoming)
        current = lax.dynamic_index_in_dim(state[1], micro_slot, 0, keepdims=False)
        valid_mask = lax.dynamic_index_in_dim(valid_micro, micro_slot, 0, keepdims=False)
        stored = ()

        def working(operands):
            current_arg, grad_arg, valid_arg, stored_arg = operands
            _, kept_state, residual_sum = sublayer_forward(current_arg, valid_arg)
            return sublayer_backward(current_arg, grad_arg, kept_state, residual_sum, valid_arg)

        def resting_back(operands):
            return (
                jnp.zeros((row_count, model_width), jnp.bfloat16),
                jnp.zeros((model_width, 6 * model_width), jnp.float32),
                jnp.zeros((model_width, 2 * model_width), jnp.float32),
                jnp.zeros((hidden_width,), jnp.float32),
                jnp.zeros((model_width,), jnp.float32),
                jnp.zeros((model_width,), jnp.float32),
            )

        results = lax.cond(
            active, working, resting_back, (current, grad_output, valid_mask, stored)
        )
        totals = jax.tree.map(jnp.add, totals, tuple(results[1:]))
        grads_buffer = store_slot(grads_buffer, results[0], micro_slot, active)
        return ((totals, grads_buffer), results[0])

    def backward_scan(carry, round_index):
        inner, incoming = carry
        inner, back_current = backward_round(inner, round_index, incoming)
        incoming = shifted(back_current, "section", -1)
        return ((inner, incoming), None)

    totals = (
        jnp.zeros((model_width, 6 * model_width), jnp.float32),
        jnp.zeros((model_width, 2 * model_width), jnp.float32),
        jnp.zeros((hidden_width,), jnp.float32),
        jnp.zeros((model_width,), jnp.float32),
        jnp.zeros((model_width,), jnp.float32),
    )
    grads_buffer = jnp.zeros((micro_count, row_count, model_width), jnp.bfloat16)
    (inner, incoming), _ = lax.scan(
        backward_scan, ((totals, grads_buffer), empty_rows), jnp.arange(round_count - 1)
    )
    (totals, grads_buffer), _ = backward_round(inner, round_count - 1, incoming)
    own_grads, sent_grads, bias_grads, scale_grads, shift_grads = totals
    attention_mask = is_attention.astype(jnp.float32)
    arrived = shifted(sent_grads.astype(jnp.bfloat16), "section", -1).astype(sent_grads.dtype)
    own_grads = own_grads.at[:, 4 * model_width :].add(attention_mask * arrived)
    own_part, bias_part, scale_part, shift_part = (
        lax.psum_scatter(own_grads, "dp", scatter_dimension=0, tiled=True),
        lax.psum_scatter(bias_grads, "dp", scatter_dimension=0, tiled=True),
        lax.psum_scatter(scale_grads, "dp", scatter_dimension=0, tiled=True),
        lax.psum_scatter(shift_grads, "dp", scatter_dimension=0, tiled=True),
    )
    section_out = state[0].reshape(1, molecules, length, model_width)
    section_grad = grads_buffer.reshape(1, molecules, length, model_width)
    return (
        section_out,
        section_grad,
        own_part[None],
        bias_part[None],
        scale_part[None],
        shift_part[None],
    )


def solution(mesh):
    placed = (
        P("dp", None, None),
        P("dp", None, None),
        P("dp"),
        P("dp", None),
        P("section", None, None),
        P("section", None),
        P("section", None),
        P("section", None),
        P(),
    )
    return jax.shard_map(
        shards,
        mesh=mesh,
        in_specs=placed,
        out_specs=(
            P("section", "dp", None, None),
            P("section", "dp", None, None),
            P("section", "dp", None),
            P("section", "dp"),
            P("section", "dp"),
            P("section", "dp"),
        ),
        check_vma=False,
    )
```

profile of v0, /device:TPU:2, one launch (start us, length us, event | category | flops | bytes accessed | tf_op | source)
XLA Modules:
  0.0 1284.8 jit_solution(7687883482962426129)
XLA Ops:
  17.7 46.4 %collective-permute-done.2 = bf16[768,1536]{1,0:T(8,128)(2,1)} collective-permute-done((bf16[768,1536]{1,0:T(8,128)(2,1)S(1)}, bf16[768,1536]{1,0:T(8,128)(2,1)}, u32[]{:S(2)}, u32[]{:S(2)}) %collective-permute-start.2) | collective-permute-done | bytes 2359328 | tf_op jit(solution)/shard_map/ppermute | solution.py:16
  72.0 209.6 %while.42 = (s32[]{:T(128)}, bf16[6,202,768]{2,1,0:T(8,128)(2,1)}, bf16[6,202,768]{2,1,0:T(8,128)(2,1)}, bf16[202,768]{1,0:T(8,128)(2,1)S(1)}, s32[8]{0:T(128)},...) while((s32[]{:T(128)}, bf16[6,202,768]{2,1,0:T(8,128)(2,1)}, ...), condition=%wide.region_10.11_spmd.clone, body=%wide.region_0.10_spmd.clone.sunk | while | flops 1949441536 | bytes 26345600 | solution.py:233
  261.1 15.7 %collective-permute-start = (bf16[202,768]{1,0:T(8,128)(2,1)}, bf16[202,768]{1,0:T(8,128)(2,1)S(1)}, u32[]{:S(2)}, u32[]{:S(2)}) collective-permute-start(bf16[202,768]{1,0:T(8,128)(2,1)} %get-tuple-element.1961), channel_id=1, source_target_pairs={{0,8},{8,16},{16,24},{1,9},{9,17},{17,25},{2,10},{10,18},{18,26},{... | collective-permute-start | bytes 930824 | tf_op jit(solution)/shard_map/while/body/eval_jaxpr/ppermute | solution.py:16
  286.0 714.3 %while.43 = (s32[]{:T(128)}, f32[768,4608]{0,1:T(8,128)}, f32[768,1536]{1,0:T(8,128)}, f32[3072]{0:T(1024)}, f32[768]{0:T(1024)}, /*index=5*/f32[768]{0:T(1024)}...) while((s32[]{:T(128)}, f32[768,4608]{0,1:T(8,128)}, ...), condition=%wide.region_45.47_spmd.clone, body=%wide.region_20.46_spmd.clone.sunk | while | flops 5864094208 | bytes 268795744 | solution.py:283
  338.8 15.8 %select_add_fusion.9 = f32[768,4608]{0,1:T(8,128)} fusion(f32[768,4608]{0,1:T(8,128)} %get-tuple-element.1756, f32[768,4608]{0,1:T(8,128)} %get-tuple-element.1897, pred[]{:T(512)S(6)} %compare.15), kind=kLoop, calls=%fused_computation.492.clone.1 | loop fusion | flops 7077888 | bytes 42467328 | tf_op jit(solution)/shard_map/while/body/eval_jaxpr/add | solution.py:265
  362.0 77.9 %collective-permute-done.1 = bf16[202,768]{1,0:T(8,128)(2,1)S(1)} collective-permute-done((bf16[202,768]{1,0:T(8,128)(2,1)}, bf16[202,768]{1,0:T(8,128)(2,1)S(1)}, u32[]{:S(2)}, u32[]{:S(2)}) %collective-permute-start.1) | collective-permute-done | bytes 310304 | tf_op jit(solution)/shard_map/while/body/eval_jaxpr/ppermute | solution.py:16
  442.1 60.1 %conditional.55 = (bf16[202,768]{1,0:T(8,128)(2,1)}, f32[768,4608]{0,1:T(8,128)}, f32[768,1536]{1,0:T(8,128)}, f32[3072]{0:T(1024)}, f32[768]{0:T(1024)}, /*index=5*/f32[768]{0:T(1024)}) conditional(s32[]{:T(128)} %convert_element_type.404, () %tuple.275, (pred[]{:T(512)}, bf16[6,202,768]{2,1,0:T(8,128)(2,1)}, s32[]{:T(128)}, ...), branch_computations={%region_21.21_spmd, %region_22.45_spmd} | conditional | flops 5854490112 | bytes 176122448 | solution.py:262
  458.6 41.0 %conditional.48 = (f32[768,4608]{0,1:T(8,128)}, f32[768,1536]{1,0:T(8,128)}, f32[3072]{0:T(1024)}, f32[768]{0:T(1024)}, f32[768]{0:T(1024)}, /*index=5*/bf16[202,768]{1,0:T(8,128)(2,1)}) conditional(s32[]{:T(128)} %convert_element_type.201, (f32[202,3072]{1,0:T(8,128)}, bf16[202,768]{1,0:T(8,128)(2,1)S(1)}, f32[1,768]{1,0:T(1,128)S(1)}, ...), branch_computations={%region_26.32_spmd, %region_34.44_spmd} | conditional | flops 3906757632 | bytes 140039888
  504.2 15.8 %select_add_fusion.9 = f32[768,4608]{0,1:T(8,128)} fusion(f32[768,4608]{0,1:T(8,128)} %get-tuple-element.1756, f32[768,4608]{0,1:T(8,128)} %get-tuple-element.1897, pred[]{:T(512)S(6)} %compare.15), kind=kLoop, calls=%fused_computation.492.clone.1 | loop fusion | flops 7077888 | bytes 42467328 | tf_op jit(solution)/shard_map/while/body/eval_jaxpr/add | solution.py:265
  534.8 60.1 %conditional.55 = (bf16[202,768]{1,0:T(8,128)(2,1)}, f32[768,4608]{0,1:T(8,128)}, f32[768,1536]{1,0:T(8,128)}, f32[3072]{0:T(1024)}, f32[768]{0:T(1024)}, /*index=5*/f32[768]{0:T(1024)}) conditional(s32[]{:T(128)} %convert_element_type.404, () %tuple.275, (pred[]{:T(512)}, bf16[6,202,768]{2,1,0:T(8,128)(2,1)}, s32[]{:T(128)}, ...), branch_computations={%region_21.21_spmd, %region_22.45_spmd} | conditional | flops 5854490112 | bytes 176122448 | solution.py:262
  551.3 40.8 %conditional.48 = (f32[768,4608]{0,1:T(8,128)}, f32[768,1536]{1,0:T(8,128)}, f32[3072]{0:T(1024)}, f32[768]{0:T(1024)}, f32[768]{0:T(1024)}, /*index=5*/bf16[202,768]{1,0:T(8,128)(2,1)}) conditional(s32[]{:T(128)} %convert_element_type.201, (f32[202,3072]{1,0:T(8,128)}, bf16[202,768]{1,0:T(8,128)(2,1)S(1)}, f32[1,768]{1,0:T(1,128)S(1)}, ...), branch_computations={%region_26.32_spmd, %region_34.44_spmd} | conditional | flops 3906757632 | bytes 140039888
  596.9 15.8 %select_add_fusion.9 = f32[768,4608]{0,1:T(8,128)} fusion(f32[768,4608]{0,1:T(8,128)} %get-tuple-element.1756, f32[768,4608]{0,1:T(8,128)} %get-tuple-element.1897, pred[]{:T(512)S(6)} %compare.15), kind=kLoop, calls=%fused_computation.492.clone.1 | loop fusion | flops 7077888 | bytes 42467328 | tf_op jit(solution)/shard_map/while/body/eval_jaxpr/add | solution.py:265
  627.4 60.1 %conditional.55 = (bf16[202,768]{1,0:T(8,128)(2,1)}, f32[768,4608]{0,1:T(8,128)}, f32[768,1536]{1,0:T(8,128)}, f32[3072]{0:T(1024)}, f32[768]{0:T(1024)}, /*index=5*/f32[768]{0:T(1024)}) conditional(s32[]{:T(128)} %convert_element_type.404, () %tuple.275, (pred[]{:T(512)}, bf16[6,202,768]{2,1,0:T(8,128)(2,1)}, s32[]{:T(128)}, ...), branch_computations={%region_21.21_spmd, %region_22.45_spmd} | conditional | flops 5854490112 | bytes 176122448 | solution.py:262
  643.8 41.0 %conditional.48 = (f32[768,4608]{0,1:T(8,128)}, f32[768,1536]{1,0:T(8,128)}, f32[3072]{0:T(1024)}, f32[768]{0:T(1024)}, f32[768]{0:T(1024)}, /*index=5*/bf16[202,768]{1,0:T(8,128)(2,1)}) conditional(s32[]{:T(128)} %convert_element_type.201, (f32[202,3072]{1,0:T(8,128)}, bf16[202,768]{1,0:T(8,128)(2,1)S(1)}, f32[1,768]{1,0:T(1,128)S(1)}, ...), branch_computations={%region_26.32_spmd, %region_34.44_spmd} | conditional | flops 3906757632 | bytes 140039888
  689.4 15.8 %select_add_fusion.9 = f32[768,4608]{0,1:T(8,128)} fusion(f32[768,4608]{0,1:T(8,128)} %get-tuple-element.1756, f32[768,4608]{0,1:T(8,128)} %get-tuple-element.1897, pred[]{:T(512)S(6)} %compare.15), kind=kLoop, calls=%fused_computation.492.clone.1 | loop fusion | flops 7077888 | bytes 42467328 | tf_op jit(solution)/shard_map/while/body/eval_jaxpr/add | solution.py:265
  720.1 60.1 %conditional.55 = (bf16[202,768]{1,0:T(8,128)(2,1)}, f32[768,4608]{0,1:T(8,128)}, f32[768,1536]{1,0:T(8,128)}, f32[3072]{0:T(1024)}, f32[768]{0:T(1024)}, /*index=5*/f32[768]{0:T(1024)}) conditional(s32[]{:T(128)} %convert_element_type.404, () %tuple.275, (pred[]{:T(512)}, bf16[6,202,768]{2,1,0:T(8,128)(2,1)}, s32[]{:T(128)}, ...), branch_computations={%region_21.21_spmd, %region_22.45_spmd} | conditional | flops 5854490112 | bytes 176122448 | solution.py:262
  721.2 14.4 %conditional.30 = (f32[202,3072]{1,0:T(8,128)}, f32[202,768]{1,0:T(8,128)S(1)}) conditional(s32[]{:T(128)} %convert_element_type.201, (bf16[768,4608]{1,0:T(8,128)(2,1)}, bf16[202,768]{1,0:T(8,128)(2,1)S(1)}, f32[1,3072]{1,0:T(1,128)}, bf16[768,3072]{1,0:T(8,128)(2,1)}) %tuple.125, (bf16[768,4608]{1,0:T(8,128)(2,1)}, ...), branch_computations={%region_23.22_spmd, %region_24.24_spmd} | conditional | flops 1947577344 | bytes 34529324 | solution.py:120
  736.6 40.8 %conditional.48 = (f32[768,4608]{0,1:T(8,128)}, f32[768,1536]{1,0:T(8,128)}, f32[3072]{0:T(1024)}, f32[768]{0:T(1024)}, f32[768]{0:T(1024)}, /*index=5*/bf16[202,768]{1,0:T(8,128)(2,1)}) conditional(s32[]{:T(128)} %convert_element_type.201, (f32[202,3072]{1,0:T(8,128)}, bf16[202,768]{1,0:T(8,128)(2,1)S(1)}, f32[1,768]{1,0:T(1,128)S(1)}, ...), branch_computations={%region_26.32_spmd, %region_34.44_spmd} | conditional | flops 3906757632 | bytes 140039888
  782.2 15.8 %select_add_fusion.9 = f32[768,4608]{0,1:T(8,128)} fusion(f32[768,4608]{0,1:T(8,128)} %get-tuple-element.1756, f32[768,4608]{0,1:T(8,128)} %get-tuple-element.1897, pred[]{:T(512)S(6)} %compare.15), kind=kLoop, calls=%fused_computation.492.clone.1 | loop fusion | flops 7077888 | bytes 42467328 | tf_op jit(solution)/shard_map/while/body/eval_jaxpr/add | solution.py:265
  812.7 60.1 %conditional.55 = (bf16[202,768]{1,0:T(8,128)(2,1)}, f32[768,4608]{0,1:T(8,128)}, f32[768,1536]{1,0:T(8,128)}, f32[3072]{0:T(1024)}, f32[768]{0:T(1024)}, /*index=5*/f32[768]{0:T(1024)}) conditional(s32[]{:T(128)} %convert_element_type.404, () %tuple.275, (pred[]{:T(512)}, bf16[6,202,768]{2,1,0:T(8,128)(2,1)}, s32[]{:T(128)}, ...), branch_computations={%region_21.21_spmd, %region_22.45_spmd} | conditional | flops 5854490112 | bytes 176122448 | solution.py:262
  829.1 41.0 %conditional.48 = (f32[768,4608]{0,1:T(8,128)}, f32[768,1536]{1,0:T(8,128)}, f32[3072]{0:T(1024)}, f32[768]{0:T(1024)}, f32[768]{0:T(1024)}, /*index=5*/bf16[202,768]{1,0:T(8,128)(2,1)}) conditional(s32[]{:T(128)} %convert_element_type.201, (f32[202,3072]{1,0:T(8,128)}, bf16[202,768]{1,0:T(8,128)(2,1)S(1)}, f32[1,768]{1,0:T(1,128)S(1)}, ...), branch_computations={%region_26.32_spmd, %region_34.44_spmd} | conditional | flops 3906757632 | bytes 140039888
  874.7 15.8 %select_add_fusion.9 = f32[768,4608]{0,1:T(8,128)} fusion(f32[768,4608]{0,1:T(8,128)} %get-tuple-element.1756, f32[768,4608]{0,1:T(8,128)} %get-tuple-element.1897, pred[]{:T(512)S(6)} %compare.15), kind=kLoop, calls=%fused_computation.492.clone.1 | loop fusion | flops 7077888 | bytes 42467328 | tf_op jit(solution)/shard_map/while/body/eval_jaxpr/add | solution.py:265
  905.4 60.1 %conditional.55 = (bf16[202,768]{1,0:T(8,128)(2,1)}, f32[768,4608]{0,1:T(8,128)}, f32[768,1536]{1,0:T(8,128)}, f32[3072]{0:T(1024)}, f32[768]{0:T(1024)}, /*index=5*/f32[768]{0:T(1024)}) conditional(s32[]{:T(128)} %convert_element_type.404, () %tuple.275, (pred[]{:T(512)}, bf16[6,202,768]{2,1,0:T(8,128)(2,1)}, s32[]{:T(128)}, ...), branch_computations={%region_21.21_spmd, %region_22.45_spmd} | conditional | flops 5854490112 | bytes 176122448 | solution.py:262
  906.5 14.4 %conditional.30 = (f32[202,3072]{1,0:T(8,128)}, f32[202,768]{1,0:T(8,128)S(1)}) conditional(s32[]{:T(128)} %convert_element_type.201, (bf16[768,4608]{1,0:T(8,128)(2,1)}, bf16[202,768]{1,0:T(8,128)(2,1)S(1)}, f32[1,3072]{1,0:T(1,128)}, bf16[768,3072]{1,0:T(8,128)(2,1)}) %tuple.125, (bf16[768,4608]{1,0:T(8,128)(2,1)}, ...), branch_computations={%region_23.22_spmd, %region_24.24_spmd} | conditional | flops 1947577344 | bytes 34529324 | solution.py:120
  921.9 40.8 %conditional.48 = (f32[768,4608]{0,1:T(8,128)}, f32[768,1536]{1,0:T(8,128)}, f32[3072]{0:T(1024)}, f32[768]{0:T(1024)}, f32[768]{0:T(1024)}, /*index=5*/bf16[202,768]{1,0:T(8,128)(2,1)}) conditional(s32[]{:T(128)} %convert_element_type.201, (f32[202,3072]{1,0:T(8,128)}, bf16[202,768]{1,0:T(8,128)(2,1)S(1)}, f32[1,768]{1,0:T(1,128)S(1)}, ...), branch_computations={%region_26.32_spmd, %region_34.44_spmd} | conditional | flops 3906757632 | bytes 140039888
  967.5 15.8 %select_add_fusion.9 = f32[768,4608]{0,1:T(8,128)} fusion(f32[768,4608]{0,1:T(8,128)} %get-tuple-element.1756, f32[768,4608]{0,1:T(8,128)} %get-tuple-element.1897, pred[]{:T(512)S(6)} %compare.15), kind=kLoop, calls=%fused_computation.492.clone.1 | loop fusion | flops 7077888 | bytes 42467328 | tf_op jit(solution)/shard_map/while/body/eval_jaxpr/add | solution.py:265
  1000.3 17.9 %conditional.38 = (bf16[202,768]{1,0:T(8,128)(2,1)}, f32[768,1536]{1,0:T(8,128)}, f32[3072]{0:T(1024)}, f32[768]{0:T(1024)}, f32[768]{0:T(1024)}, /*index=5*/f32[768,4608]{1,0:T(8,128)}) conditional(s32[]{:T(128)} %convert_element_type.237, () %tuple.155, (pred[]{:T(512)}, bf16[6,202,768]{2,1,0:T(8,128)(2,1)}, s32[]{:T(128)}, f32[6,202]{1,0:T(8,128)}, ...), branch_computations={%region_46.48_spmd, %region_47.71_spmd} | conditional | flops 5854490112 | bytes 252074640 | solution.py:262
  1022.7 63.4 %collective-permute-start.3 = (bf16[768,1536]{1,0:T(8,128)(2,1)S(1)}, bf16[768,1536]{1,0:T(8,128)(2,1)}, u32[]{:S(2)}, u32[]{:S(2)}) collective-permute-start(bf16[768,1536]{1,0:T(8,128)(2,1)S(1)} %add_convert_fusion.16), channel_id=1, source_target_pairs={{8,0},{16,8},{24,16},{9,1},{17,9},{25,17},{10,2},{18,10},{26,18},{... | collective-permute-start | bytes 7077896 | tf_op jit(solution)/shard_map/ppermute | solution.py:16
  1086.1 15.1 %copy.83 = f32[768,4608]{1,0:T(8,128)} copy(f32[768,4608]{0,1:T(8,128)} %get-tuple-element.1124) | data formatting | bytes 28311552 | tf_op jit(solution)/shard_map/while | solution.py:283
  1101.2 15.3 %add.408 = f32[768,4608]{1,0:T(8,128)} add(f32[768,4608]{1,0:T(8,128)} %copy.83, f32[768,4608]{1,0:T(8,128)} %get-tuple-element.1346) | non-fusion elementwise | flops 3538944 | bytes 42467328 | tf_op jit(solution)/shard_map/add | solution.py:265
  1136.0 27.1 %all-reduce.9 = (f32[3072]{0:T(1024)S(1)}, f32[768]{0:T(1024)}, f32[768]{0:T(1024)}) all-reduce(f32[3072]{0:T(1024)S(1)} %add.411, f32[768]{0:T(1024)S(1)} %add.412, f32[768]{0:T(1024)S(1)} %add.413), channel_id=3, replica_groups=mesh['section'=4,'dp'=8] {'dp'}, use_global_device_ids=true, to_apply=%region_71.73.clone | all-reduce | flops 4608 | bytes 36864
  1171.5 106.1 %reduce-scatter.2.cloned.1.call-done = f32[96,4608]{1,0:T(8,128)} async-done(((f32[768,4608]{1,0:T(8,128)}), f32[96,4608]{1,0:T(8,128)}) %reduce-scatter.2.cloned.1.call-update) | async-done | bytes 1769488 | tf_op jit(solution)/shard_map/reduce_scatter | solution.py:292
  (643 shorter events, 961.8 us)
Async XLA Ops:
  7.2 1270.5 %reduce-scatter.2.cloned.1.call-start = ((), (), s32[]{:S(2)}) async-start(), calls=%async_computation.1 | async-start | bytes 15925248 | tf_op jit(solution)/shard_map/reduce_scatter | solution.py:292
  9.1 55.0 %collective-permute-start.2 = (bf16[768,1536]{1,0:T(8,128)(2,1)S(1)}, bf16[768,1536]{1,0:T(8,128)(2,1)}, u32[]{:S(2)}, u32[]{:S(2)}) collective-permute-start(bf16[768,1536]{1,0:T(8,128)(2,1)S(1)} %slice.223), channel_id=1, source_target_pairs={{0,8},{8,16},{16,24},{1,9},{9,17},{17,25},{2,10},{10,18},{18,26},{... | collective-permute-start | bytes 7077896 | tf_op jit(solution)/shard_map/ppermute | solution.py:16
  78.2 18.1 %collective-permute-start = (bf16[202,768]{1,0:T(8,128)(2,1)}, bf16[202,768]{1,0:T(8,128)(2,1)S(1)}, u32[]{:S(2)}, u32[]{:S(2)}) collective-permute-start(bf16[202,768]{1,0:T(8,128)(2,1)} %get-tuple-element.1961), channel_id=1, source_target_pairs={{0,8},{8,16},{16,24},{1,9},{9,17},{17,25},{2,10},{10,18},{18,26},{... | collective-permute-start | bytes 930824 | tf_op jit(solution)/shard_map/while/body/eval_jaxpr/ppermute | solution.py:16
  113.5 9.8 collective-permute-start
  140.4 9.1 collective-permute-start
  166.6 9.1 collective-permute-start
  192.8 9.1 collective-permute-start
  219.0 9.2 collective-permute-start
  245.3 9.6 collective-permute-start
  261.1 20.6 %collective-permute-start = (bf16[202,768]{1,0:T(8,128)(2,1)}, bf16[202,768]{1,0:T(8,128)(2,1)S(1)}, u32[]{:S(2)}, u32[]{:S(2)}) collective-permute-start(bf16[202,768]{1,0:T(8,128)(2,1)} %get-tuple-element.1961), channel_id=1, source_target_pairs={{0,8},{8,16},{16,24},{1,9},{9,17},{17,25},{2,10},{10,18},{18,26},{... | collective-permute-start | bytes 930824 | tf_op jit(solution)/shard_map/while/body/eval_jaxpr/ppermute | solution.py:16
  302.2 21.0 %collective-permute-start.1 = (bf16[202,768]{1,0:T(8,128)(2,1)}, bf16[202,768]{1,0:T(8,128)(2,1)S(1)}, u32[]{:S(2)}, u32[]{:S(2)}) collective-permute-start(bf16[202,768]{1,0:T(8,128)(2,1)} %get-tuple-element.1763), channel_id=1, source_target_pairs={{8,0},{16,8},{24,16},{9,1},{17,9},{25,17},{10,2},{18,10},{26,18},{... | collective-permute-start | bytes 930824 | tf_op jit(solution)/shard_map/while/body/eval_jaxpr/ppermute | solution.py:16
  336.8 103.0 %collective-permute-start.1 = (bf16[202,768]{1,0:T(8,128)(2,1)}, bf16[202,768]{1,0:T(8,128)(2,1)S(1)}, u32[]{:S(2)}, u32[]{:S(2)}) collective-permute-start(bf16[202,768]{1,0:T(8,128)(2,1)} %get-tuple-element.1763), channel_id=1, source_target_pairs={{8,0},{16,8},{24,16},{9,1},{17,9},{25,17},{10,2},{18,10},{26,18},{... | collective-permute-start | bytes 930824 | tf_op jit(solution)/shard_map/while/body/eval_jaxpr/ppermute | solution.py:16
  338.8 15.8 %slice-start = ((s8[4718592]{0:T(1024)(128)(4,1)}), s8[4194304]{0:T(1024)(128)(4,1)S(1)}, s32[]{:S(2)}) async-start(s8[4718592]{0:T(1024)(128)(4,1)} %bitcast.601), calls=%async_computation.2 | async-start | bytes 8388608 | tf_op jit(solution)/shard_map/while
  354.6 85.3 %copy-start.46 = (s32[8]{0:T(128)S(1)}, s32[8]{0:T(128)}, u32[]{:S(2)}) copy-start(s32[8]{0:T(128)} %copy-done.45) | copy-start | bytes 100 | tf_op jit(solution)/shard_map/while
  358.6 81.3 %copy-start.1 = (f32[768,1536]{1,0:T(8,128)}, f32[768,1536]{1,0:T(8,128)S(1)}, u32[]{:S(2)}) copy-start(f32[768,1536]{1,0:T(8,128)S(1)} %select_add_fusion.10) | copy-start | bytes 14155780 | tf_op jit(solution)/shard_map/while
  359.3 80.5 %copy-start.29 = (f32[3072]{0:T(1024)}, f32[3072]{0:T(1024)S(1)}, u32[]{:S(2)}) copy-start(f32[3072]{0:T(1024)S(1)} %select_add_fusion.11) | copy-start | bytes 36868 | tf_op jit(solution)/shard_map/while
  360.1 79.8 %copy-start.38 = (f32[768]{0:T(1024)}, f32[768]{0:T(1024)S(1)}, u32[]{:S(2)}) copy-start(f32[768]{0:T(1024)S(1)} %get-tuple-element.1925) | copy-start | bytes 9220 | tf_op jit(solution)/shard_map/while
  360.1 79.8 %copy-start.41 = (f32[768]{0:T(1024)}, f32[768]{0:T(1024)S(1)}, u32[]{:S(2)}) copy-start(f32[768]{0:T(1024)S(1)} %get-tuple-element.1926) | copy-start | bytes 9220 | tf_op jit(solution)/shard_map/while
  502.2 30.1 %collective-permute-start.1 = (bf16[202,768]{1,0:T(8,128)(2,1)}, bf16[202,768]{1,0:T(8,128)(2,1)S(1)}, u32[]{:S(2)}, u32[]{:S(2)}) collective-permute-start(bf16[202,768]{1,0:T(8,128)(2,1)} %get-tuple-element.1763), channel_id=1, source_target_pairs={{8,0},{16,8},{24,16},{9,1},{17,9},{25,17},{10,2},{18,10},{26,18},{... | collective-permute-start | bytes 930824 | tf_op jit(solution)/shard_map/while/body/eval_jaxpr/ppermute | solution.py:16
  504.2 15.8 %slice-start = ((s8[4718592]{0:T(1024)(128)(4,1)}), s8[4194304]{0:T(1024)(128)(4,1)S(1)}, s32[]{:S(2)}) async-start(s8[4718592]{0:T(1024)(128)(4,1)} %bitcast.601), calls=%async_computation.2 | async-start | bytes 8388608 | tf_op jit(solution)/shard_map/while
  595.0 30.2 %collective-permute-start.1 = (bf16[202,768]{1,0:T(8,128)(2,1)}, bf16[202,768]{1,0:T(8,128)(2,1)S(1)}, u32[]{:S(2)}, u32[]{:S(2)}) collective-permute-start(bf16[202,768]{1,0:T(8,128)(2,1)} %get-tuple-element.1763), channel_id=1, source_target_pairs={{8,0},{16,8},{24,16},{9,1},{17,9},{25,17},{10,2},{18,10},{26,18},{... | collective-permute-start | bytes 930824 | tf_op jit(solution)/shard_map/while/body/eval_jaxpr/ppermute | solution.py:16
  596.9 15.8 %slice-start = ((s8[4718592]{0:T(1024)(128)(4,1)}), s8[4194304]{0:T(1024)(128)(4,1)S(1)}, s32[]{:S(2)}) async-start(s8[4718592]{0:T(1024)(128)(4,1)} %bitcast.601), calls=%async_computation.2 | async-start | bytes 8388608 | tf_op jit(solution)/shard_map/while
  687.5 30.2 %collective-permute-start.1 = (bf16[202,768]{1,0:T(8,128)(2,1)}, bf16[202,768]{1,0:T(8,128)(2,1)S(1)}, u32[]{:S(2)}, u32[]{:S(2)}) collective-permute-start(bf16[202,768]{1,0:T(8,128)(2,1)} %get-tuple-element.1763), channel_id=1, source_target_pairs={{8,0},{16,8},{24,16},{9,1},{17,9},{25,17},{10,2},{18,10},{26,18},{... | collective-permute-start | bytes 930824 | tf_op jit(solution)/shard_map/while/body/eval_jaxpr/ppermute | solution.py:16
  689.4 15.8 %slice-start = ((s8[4718592]{0:T(1024)(128)(4,1)}), s8[4194304]{0:T(1024)(128)(4,1)S(1)}, s32[]{:S(2)}) async-start(s8[4718592]{0:T(1024)(128)(4,1)} %bitcast.601), calls=%async_computation.2 | async-start | bytes 8388608 | tf_op jit(solution)/shard_map/while
  780.2 30.2 %collective-permute-start.1 = (bf16[202,768]{1,0:T(8,128)(2,1)}, bf16[202,768]{1,0:T(8,128)(2,1)S(1)}, u32[]{:S(2)}, u32[]{:S(2)}) collective-permute-start(bf16[202,768]{1,0:T(8,128)(2,1)} %get-tuple-element.1763), channel_id=1, source_target_pairs={{8,0},{16,8},{24,16},{9,1},{17,9},{25,17},{10,2},{18,10},{26,18},{... | collective-permute-start | bytes 930824 | tf_op jit(solution)/shard_map/while/body/eval_jaxpr/ppermute | solution.py:16
  782.2 15.8 %slice-start = ((s8[4718592]{0:T(1024)(128)(4,1)}), s8[4194304]{0:T(1024)(128)(4,1)S(1)}, s32[]{:S(2)}) async-start(s8[4718592]{0:T(1024)(128)(4,1)} %bitcast.601), calls=%async_computation.2 | async-start | bytes 8388608 | tf_op jit(solution)/shard_map/while
  872.8 30.2 %collective-permute-start.1 = (bf16[202,768]{1,0:T(8,128)(2,1)}, bf16[202,768]{1,0:T(8,128)(2,1)S(1)}, u32[]{:S(2)}, u32[]{:S(2)}) collective-permute-start(bf16[202,768]{1,0:T(8,128)(2,1)} %get-tuple-element.1763), channel_id=1, source_target_pairs={{8,0},{16,8},{24,16},{9,1},{17,9},{25,17},{10,2},{18,10},{26,18},{... | collective-permute-start | bytes 930824 | tf_op jit(solution)/shard_map/while/body/eval_jaxpr/ppermute | solution.py:16
  965.5 26.2 %collective-permute-start.1 = (bf16[202,768]{1,0:T(8,128)(2,1)}, bf16[202,768]{1,0:T(8,128)(2,1)S(1)}, u32[]{:S(2)}, u32[]{:S(2)}) collective-permute-start(bf16[202,768]{1,0:T(8,128)(2,1)} %get-tuple-element.1763), channel_id=1, source_target_pairs={{8,0},{16,8},{24,16},{9,1},{17,9},{25,17},{10,2},{18,10},{26,18},{... | collective-permute-start | bytes 930824 | tf_op jit(solution)/shard_map/while/body/eval_jaxpr/ppermute | solution.py:16
  1022.7 102.7 %collective-permute-start.3 = (bf16[768,1536]{1,0:T(8,128)(2,1)S(1)}, bf16[768,1536]{1,0:T(8,128)(2,1)}, u32[]{:S(2)}, u32[]{:S(2)}) collective-permute-start(bf16[768,1536]{1,0:T(8,128)(2,1)S(1)} %add_convert_fusion.16), channel_id=1, source_target_pairs={{8,0},{16,8},{24,16},{9,1},{17,9},{25,17},{10,2},{18,10},{26,18},{... | collective-permute-start | bytes 7077896 | tf_op jit(solution)/shard_map/ppermute | solution.py:16
  1131.4 32.4 %copy-start.11 = (bf16[6,202,768]{2,1,0:T(8,128)(2,1)S(1)}, bf16[6,202,768]{2,1,0:T(8,128)(2,1)}, u32[]{:S(2)}) copy-start(bf16[6,202,768]{2,1,0:T(8,128)(2,1)} %get-tuple-element.1121) | copy-start | bytes 5584900
  1131.4 33.6 %copy-start.32 = (f32[1,768]{1,0:T(1,128)S(1)}, f32[1,768]{1,0:T(1,128)}, u32[]{:S(2)}) copy-start(f32[1,768]{1,0:T(1,128)} %param.43) | copy-start | bytes 9220
  1131.4 33.6 %copy-start.33 = (bf16[202,768]{1,0:T(8,128)(2,1)S(1)}, bf16[202,768]{1,0:T(8,128)(2,1)}, u32[]{:S(2)}) copy-start(bf16[202,768]{1,0:T(8,128)(2,1)} %get-tuple-element.1457) | copy-start | bytes 930820
  (111 other events, 701.9 us)
Sparse Core Ops, SparseCore 0:
  1131.5 146.0 reduce-scatter.1
where the time goes:
time: 1300 us; the launch traced here: 1280 us
  other arithmetic  314 us (24%)
  waiting for transfers between devices  292 us (22%)
  matrix products  275 us (21%)
  local copies, waits for them, and re-layouts  180 us (14%)
  starting transfers between devices  123 us (9%)
  loops' own time  56.5 us (4%)
  blocking collectives  27.1 us (2%)
  between operations  15.8 us (1%)
    ppermute x18, waiting for transfers between devices, shifted(): return lax.ppermute(array, axis, pairs)  186 us
    add x36, other arithmetic, backward_round(): totals = jax.tree.map(jnp.add, totals, tuple(results[1:]))  183 us
    dot_general x18, matrix products, contract_cols(): lax.dot_general(left, right, (((1,), (1,)), ((), ())), preferred_element_...  132 us
    ppermute x18, starting transfers between devices, shifted(): return lax.ppermute(array, axis, pairs)  123 us
    reduce_scatter x1, waiting for transfers between devices, shards(): lax.psum_scatter(own_grads, 'dp', scatter_dimension=0, tiled=True)  106 us
    dot_general x12, matrix products, contract_rows(): lax.dot_general(left, right, (((0,), (0,)), ((), ())), preferred_element_...  56.5 us
    dot_general x6, matrix products, feed_backward(): jnp.dot(back_branch, down_full, preferred_element_type=jnp.float32)  55.8 us
    unnamed x70, local copies, waits for them, and re-layouts  45.8 us
  transfers between devices with their start and end apart: 19, of which 17 were waited for; matrix products, arithmetic and copies ran while one was open for 20% of the time, Pallas kernels for 0%

commit v1 on v0

v1 whole, which is shorter than its diff:
```python
import functools

import jax
import jax.numpy as jnp
from jax import lax
from jax.experimental import pallas as pl
from jax.experimental.pallas import tpu as pltpu
from jax.sharding import PartitionSpec as P

MESH = pl.DeviceIdType.MESH
norm_epsilon = 1e-05
bf16 = jnp.bfloat16
f32 = jnp.float32


def dot(a, b):
    return lax.dot_general(a, b, (((1,), (0,)), ((), ())), preferred_element_type=f32)


def dot_cols(a, b):
    return lax.dot_general(a, b, (((1,), (1,)), ((), ())), preferred_element_type=f32)


def dot_rows(a, b):
    return lax.dot_general(a, b, (((0,), (0,)), ((), ())), preferred_element_type=f32)


def softplus(u):
    return jnp.maximum(u, 0.0) + jnp.log1p(jnp.exp(-jnp.abs(u)))


def block_mask(feature_rows, value_cols, features, head_dim):
    r = lax.broadcasted_iota(jnp.int32, (feature_rows, value_cols), 0) // features
    c = lax.broadcasted_iota(jnp.int32, (feature_rows, value_cols), 1) // head_dim
    return r == c


def pipeline_kernel(
    cfg,
    len_ref,
    x_hbm,
    cot_hbm,
    pred_ref,
    slab_hbm,
    bias_ref,
    gain_ref,
    shift_ref,
    fmap_ref,
    out_hbm,
    grad_hbm,
    g1_hbm,
    g2_hbm,
    bias_grad_ref,
    gain_grad_ref,
    shift_grad_ref,
    w,
    u,
    xin,
    out,
    dyin,
    dxo,
    dbr,
    nbuf,
    rbuf,
    buf_a,
    buf_b,
    szbuf,
    stage,
    land,
    load_sem,
    x_sem,
    cot_sem,
    u_send,
    u_recv,
    f_send,
    f_recv,
    b_send,
    b_recv,
    out_sem,
    grad_sem,
    g_sem,
):
    M, L, LP, D, FF, HD, FE, NS, ND, fscale = cfg
    HALF = FF // 2
    GH = 256 // HD
    G = D // 256
    GF = GH * FE
    s = lax.axis_index("section")
    d = lax.axis_index("dp")
    odd = lax.rem(s, 2)
    is_attn = odd == 0
    is_ff = odd == 1
    first = s == 0
    last = s == NS - 1
    sib = d + 1 - 2 * lax.rem(d, 2)
    mate = d + 2 - 4 * lax.rem(d // 2, 2)
    quarter = D // 4

    barrier = pltpu.get_barrier_semaphore()

    def greet(cond, ts, td):
        @pl.when(cond)
        def _():
            pl.semaphore_signal(barrier, inc=1, device_id=(ts, td), device_id_type=MESH)

    always = s >= 0
    greet(always, s, sib)
    greet(always, s, mate)
    greet(s > 0, s - 1, d)
    greet(s < NS - 1, s + 1, d)

    w_copy = pltpu.make_async_copy(slab_hbm.at[0, :, pl.ds(0, FF)], w, load_sem.at[0])
    u_copy = pltpu.make_async_copy(
        slab_hbm.at[0, :, pl.ds(FF, HALF)], u.at[:, pl.ds(HALF, HALF)], load_sem.at[1]
    )
    w_copy.start()

    @pl.when(first)
    def _():
        for m in range(M):
            pltpu.make_async_copy(x_hbm.at[m], land.at[m], x_sem.at[m]).start()

    @pl.when(last)
    def _():
        for m in range(M):
            pltpu.make_async_copy(cot_hbm.at[m], land.at[m], x_sem.at[m]).start()

    @pl.when(is_ff)
    def _():
        u_copy.start()

    bias_grad_ref[...] = jnp.zeros_like(bias_grad_ref)
    gain_grad_ref[...] = jnp.zeros_like(gain_grad_ref)
    shift_grad_ref[...] = jnp.zeros_like(shift_grad_ref)

    @pl.when(first | last)
    def _():
        pl.semaphore_wait(barrier, 3)

    @pl.when((s > 0) & (s < NS - 1))
    def _():
        pl.semaphore_wait(barrier, 4)

    q0 = lax.rem(d, 4)
    q_own = pl.ds(pl.multiple_of(q0 * quarter, quarter), quarter)
    q_mate = pl.ds(pl.multiple_of((q0 + 2 - 4 * (q0 // 2)) * quarter, quarter), quarter)
    left = pl.ds(0, HALF)

    def u_from_section():
        return pltpu.make_async_remote_copy(
            slab_hbm.at[0, q_own, pl.ds(FF, HALF)],
            u.at[q_own, left],
            u_send.at[0],
            u_recv.at[0],
            device_id=(s + 1, d),
            device_id_type=MESH,
        )

    def u_copy_to(rows, k, td):
        return pltpu.make_async_remote_copy(
            u.at[rows, left],
            u.at[rows, left],
            u_send.at[k],
            u_recv.at[k],
            device_id=(s, td),
            device_id_type=MESH,
        )

    @pl.when(is_attn & (s < NS - 1))
    def _():
        u_from_section().start()

    w_copy.wait()

    @pl.when(is_ff)
    def _():
        u_from_section().wait_recv()
        u_copy_to(q_own, 1, mate).start()
        u_copy_to(q_own, 2, sib).start()
        u_copy_to(q_own, 1, mate).wait_recv()
        u_copy_to(q_mate, 3, sib).start()
        u_copy_to(q_own, 2, sib).wait_recv()
        u_copy_to(q_mate, 3, sib).wait_recv()
        u_copy.wait()

    g_row = gain_ref[...]
    b_row = shift_ref[...]
    row_id = lax.broadcasted_iota(jnp.int32, (LP, GF), 0)
    head_mask = block_mask(GF, 256, FE, HD)
    pair_mask = jnp.concatenate([head_mask, head_mask], axis=1)
    ones_cols = jnp.ones((LP, 256), bf16)

    def norm_forward(m, pre):
        mean = jnp.mean(pre, axis=-1, keepdims=True)
        cen = pre - mean
        r = lax.rsqrt(jnp.mean(cen * cen, axis=-1, keepdims=True) + norm_epsilon)
        n = cen * r
        nbuf[m] = n
        rbuf[m] = r
        out[m] = (n * g_row + b_row).astype(bf16)

    def norm_backward(m):
        dy = dyin[m].astype(f32)
        n = nbuf[m]
        dn = dy * g_row
        dyn = dy * n
        m1 = jnp.mean(dn, axis=-1, keepdims=True)
        m2 = jnp.mean(dn * n, axis=-1, keepdims=True)
        gain_grad_ref[...] += jnp.sum(dyn, axis=0, keepdims=True)
        shift_grad_ref[...] += jnp.sum(dy, axis=0, keepdims=True)
        dpre = rbuf[m] * (dn - m1 - n * m2)
        dbr[m] = dpre.astype(bf16)
        return dpre

    def attend_forward(m):
        x = xin[m]
        valid = row_id < len_ref[m]
        for g in range(G):
            cols = [pl.ds(k * D + 256 * g, 256) for k in range(3)]
            qkv = [
                (dot(x, w[:, c]) + bias_ref[:, c]).astype(bf16) for c in cols
            ]
            fq = softplus(dot(qkv[0], fmap_ref[g]) * fscale).astype(bf16)
            fk = softplus(dot(qkv[1], fmap_ref[g]) * fscale)
            fk = jnp.where(valid, fk, 0.0).astype(bf16)
            buf_a[m, :, pl.ds(256 * g, 256)] = qkv[2]
            buf_a[m, :, pl.ds(D + GF * g, GF)] = fq
            buf_a[m, :, pl.ds(D + GF * (G + g), GF)] = fk
            sz = dot_rows(fk, jnp.concatenate([qkv[2], ones_cols], axis=1))
            sz = jnp.where(pair_mask, sz, 0.0).astype(bf16)
            szbuf[m, g] = sz
            nd = dot(fq, sz)
            buf_a[m, :, pl.ds(3 * D + 256 * g, 256)] = (nd[:, :256] / nd[:, 256:]).astype(bf16)
        branch = dot_cols(buf_a[m, :, pl.ds(3 * D, D)], w[:, pl.ds(3 * D, D)])
        norm_forward(m, x.astype(f32) + (branch + bias_ref[:, pl.ds(3 * D, D)]))

    def feed_forward(m):
        x = xin[m]
        tile = 512
        for j in range(FF // tile):
            c = pl.ds(j * tile, tile)
            a = dot(x, w[:, c]) + bias_ref[:, c]
            cdf = 0.5 + 0.5 * lax.erf(a * 0.7071067811865476)
            pdf = jnp.exp(a * a * -0.5) * 0.3989422804014327
            buf_a[m, :, c] = (a * cdf).astype(bf16)
            buf_b[m, :, c] = (cdf + a * pdf).astype(bf16)
        branch = dot_cols(buf_a[m], u[...])
        norm_forward(m, x.astype(f32) + branch)

    def attend_backward(m):
        dpre = norm_backward(m)
        db = dbr[m]
        valid = row_id < len_ref[m]
        ocols = pl.ds(3 * D, D)
        bias_grad_ref[:, ocols] += jnp.sum(db.astype(f32), axis=0, keepdims=True)
        for g in range(G):
            dmix = dot(db, w[:, pl.ds(3 * D + 256 * g, 256)])
            v = buf_a[m, :, pl.ds(256 * g, 256)]
            fq = buf_a[m, :, pl.ds(D + GF * g, GF)]
            fk = buf_a[m, :, pl.ds(D + GF * (G + g), GF)]
            sz = szbuf[m, g]
            nd = dot(fq, sz)
            rden = 1.0 / nd[:, 256:]
            dnum = dmix * rden
            dden = -dnum * (nd[:, :256] * rden)
            de = jnp.concatenate([dnum, dden], axis=1).astype(bf16)
            dfq = dot_cols(de, sz)
            dsz = jnp.where(pair_mask, dot_rows(fq, de), 0.0).astype(bf16)
            dfk = dot_cols(jnp.concatenate([v, ones_cols], axis=1), dsz)
            dv = dot(fk, dsz[:, :256]).astype(bf16)
            duq = dfq * (1.0 - jnp.exp(-fq.astype(f32)))
            duk = jnp.where(valid, dfk, 0.0) * (1.0 - jnp.exp(-fk.astype(f32)))
            dq = (dot_cols(duq.astype(bf16), fmap_ref[g]) * fscale).astype(bf16)
            dk = (dot_cols(duk.astype(bf16), fmap_ref[g]) * fscale).astype(bf16)
            for k, val in enumerate((dq, dk, dv)):
                c = pl.ds(k * D + 256 * g, 256)
                buf_b[m, :, c] = val
                bias_grad_ref[:, c] += jnp.sum(val.astype(f32), axis=0, keepdims=True)
        dx = dpre + dot_cols(buf_b[m, :, pl.ds(0, 3 * D)], w[:, pl.ds(0, 3 * D)])
        dxo[m] = dx.astype(bf16)

    def feed_backward(m):
        dpre = norm_backward(m)
        db = dbr[m]
        tile = 512
        for j in range(FF // tile):
            c = pl.ds(j * tile, tile)
            da = (dot(db, u[:, c]) * buf_b[m, :, c].astype(f32)).astype(bf16)
            buf_b[m, :, c] = da
            bias_grad_ref[:, c] += jnp.sum(da.astype(f32), axis=0, keepdims=True)
        dx = dpre + dot_cols(buf_b[m], w[...])
        dxo[m] = dx.astype(bf16)

    def next_copy(m):
        return pltpu.make_async_remote_copy(
            out.at[m],
            xin.at[m],
            f_send.at[m],
            f_recv.at[m],
            device_id=(s + 1, d),
            device_id_type=MESH,
        )

    def back_copy(m):
        return pltpu.make_async_remote_copy(
            dxo.at[m],
            dyin.at[m],
            b_send.at[m],
            b_recv.at[m],
            device_id=(s - 1, d),
            device_id_type=MESH,
        )

    def out_copy(m):
        return pltpu.make_async_copy(out.at[m], out_hbm.at[m], out_sem.at[m])

    def grad_copy(m):
        return pltpu.make_async_copy(dxo.at[m], grad_hbm.at[m], grad_sem.at[m])

    def land_copy(m):
        return pltpu.make_async_copy(x_hbm.at[m], land.at[m], x_sem.at[m])

    pad_zero = jnp.zeros((LP - L, D), bf16)
    eye = lax.broadcasted_iota(jnp.int32, (L, L), 0) == lax.broadcasted_iota(jnp.int32, (L, L), 1)

    def forward_step(m):
        @pl.when(first)
        def _():
            land_copy(m).wait()
            xin[m] = jnp.concatenate([land[m], pad_zero], axis=0)

        @pl.when(s > 0)
        def _():
            next_copy(m).wait_recv()

        @pl.when(is_attn)
        def _():
            attend_forward(m)

        @pl.when(is_ff)
        def _():
            feed_forward(m)

        @pl.when(s < NS - 1)
        def _():
            next_copy(m).start()

        out_copy(m).start()

    def backward_step(m):
        @pl.when(last)
        def _():
            land_copy(m).wait()
            row = jnp.where(
                lax.broadcasted_iota(jnp.int32, (1, L), 1) < len_ref[m],
                pred_ref[pl.ds(m, 1), :].astype(f32),
                0.0,
            )
            col = jnp.sum(jnp.where(eye, row, 0.0), axis=1, keepdims=True)
            masked = (land[m].astype(f32) * col).astype(bf16)
            dyin[m] = jnp.concatenate([masked, pad_zero], axis=0)

        @pl.when(s < NS - 1)
        def _():
            back_copy(m).wait_recv()

        @pl.when(is_attn)
        def _():
            attend_backward(m)

        @pl.when(is_ff)
        def _():
            feed_backward(m)

        @pl.when(s > 0)
        def _():
            back_copy(m).start()

        grad_copy(m).start()

    back_start = 6 - (s * s) // 3

    def tick(t, carry):
        mf = t - s
        mb = t - back_start

        @pl.when((mf >= 0) & (mf < M))
        def _():
            forward_step(mf)

        @pl.when((mb >= 0) & (mb < M))
        def _():
            backward_step(mb)

        return carry

    lax.fori_loop(0, 6 + M, tick, 0)

    def flat(ref, c):
        return ref[:, :, c].reshape(M * LP, c.size)

    @pl.when(is_ff)
    def _():
        for k in range(2):
            src = (xin, dbr)[k]
            rhs = (buf_b, buf_a)[k]
            dst = (g1_hbm, g2_hbm)[k]
            for j in range(FF // D):
                c = pl.ds(j * D, D)
                if j + k > 0:
                    cp.wait()
                stage[...] = dot_rows(flat(src, pl.ds(0, D)), flat(rhs, c))
                cp = pltpu.make_async_copy(stage, dst.at[:, c], g_sem.at[0])
                cp.start()
        cp.wait()

    @pl.when(is_attn)
    def _():
        for j in range(FF // D):
            c = pl.ds(j * D, D)
            if j > 0:
                cp.wait()
            if j < 3:
                stage[...] = dot_rows(flat(xin, pl.ds(0, D)), flat(buf_b, c))
            else:
                stage[...] = dot_rows(flat(dbr, pl.ds(0, D)), flat(buf_a, c))
            cp = pltpu.make_async_copy(stage, g1_hbm.at[:, c], g_sem.at[0])
            cp.start()
        cp.wait()
        stage[...] = jnp.zeros_like(stage)
        for j in range(FF // D):
            cp = pltpu.make_async_copy(stage, g2_hbm.at[:, pl.ds(j * D, D)], g_sem.at[0])
            cp.start()
            cp.wait()

    @pl.when(is_attn & (s < NS - 1))
    def _():
        u_from_section().wait_send()

    @pl.when(is_ff)
    def _():
        u_copy_to(q_own, 1, mate).wait_send()
        u_copy_to(q_own, 2, sib).wait_send()
        u_copy_to(q_mate, 3, sib).wait_send()

    for m in range(M):
        @pl.when(s < NS - 1)
        def _():
            next_copy(m).wait_send()

        @pl.when(s > 0)
        def _():
            back_copy(m).wait_send()

        out_copy(m).wait()
        grad_copy(m).wait()


def shards(
    block_input, cotangent, lengths, predicted, slab, in_bias, norm_gain, norm_bias, feature_draws
):
    NS = lax.axis_size("section")
    ND = lax.axis_size("dp")
    M, L, D = block_input.shape
    FF = in_bias.shape[1]
    H, HD, FE = feature_draws.shape
    LP = (L + 15) // 16 * 16
    GH = 256 // HD
    G = D // 256
    GF = GH * FE
    fscale = float((3.0 / (20.0 * HD)) ** 0.5)
    draws = feature_draws.astype(bf16).reshape(G, GH, HD, FE)
    same = jnp.eye(GH, dtype=bf16)
    fmap = (draws[:, :, :, None, :] * same[None, :, None, :, None]).reshape(G, GH * HD, GF)
    cfg = (M, L, LP, D, FF, HD, FE, NS, ND, fscale)
    hbm = pl.BlockSpec(memory_space=pl.ANY)
    vmem = pl.BlockSpec(memory_space=pltpu.VMEM)
    smem = pl.BlockSpec(memory_space=pltpu.SMEM)
    dma = pltpu.SemaphoreType.DMA
    rows_bf = pltpu.VMEM((M, LP, D), bf16)
    wide_bf = pltpu.VMEM((M, LP, FF), bf16)
    outs = pl.pallas_call(
        functools.partial(pipeline_kernel, cfg),
        out_shape=[
            jax.ShapeDtypeStruct((M, LP, D), bf16),
            jax.ShapeDtypeStruct((M, LP, D), bf16),
            jax.ShapeDtypeStruct((D, FF), f32),
            jax.ShapeDtypeStruct((D, FF), f32),
            jax.ShapeDtypeStruct((1, FF), f32),
            jax.ShapeDtypeStruct((1, D), f32),
            jax.ShapeDtypeStruct((1, D), f32),
        ],
        in_specs=[smem, hbm, hbm, vmem, hbm, vmem, vmem, vmem, vmem],
        out_specs=[hbm, hbm, hbm, hbm, vmem, vmem, vmem],
        scratch_shapes=[
            pltpu.VMEM((D, FF), bf16),
            pltpu.VMEM((D, FF), bf16),
            rows_bf,
            rows_bf,
            rows_bf,
            rows_bf,
            rows_bf,
            pltpu.VMEM((M, LP, D), f32),
            pltpu.VMEM((M, LP, 1), f32),
            wide_bf,
            wide_bf,
            pltpu.VMEM((M, G, GF, 512), bf16),
            pltpu.VMEM((D, D), f32),
            pltpu.VMEM((M, L, D), bf16),
            dma((2,)),
            dma((M,)),
            dma((M,)),
            dma((4,)),
            dma((4,)),
            dma((M,)),
            dma((M,)),
            dma((M,)),
            dma((M,)),
            dma((M,)),
            dma((M,)),
            dma((1,)),
        ],
        compiler_params=pltpu.CompilerParams(
            collective_id=0, has_side_effects=True, vmem_limit_bytes=60 * 2**20
        ),
        name="pipeline",
    )(
        lengths,
        block_input,
        cotangent,
        predicted,
        slab,
        in_bias,
        norm_gain,
        norm_bias,
        fmap,
    )
    section_out, section_grad, g1, g2, bias_grad, gain_grad, shift_grad = outs
    HALF = FF // 2

    def scatter(value):
        return lax.psum_scatter(value, "dp", scatter_dimension=0, tiled=True)

    both = scatter(jnp.concatenate([g1, g2], axis=1))
    pairs = [(i, i - 1) for i in range(1, NS, 2)]
    arrived = lax.ppermute(both[:, FF : FF + HALF], "section", pairs)
    is_attention = lax.axis_index("section") % 2 == 0
    rest = jnp.where(is_attention, arrived, both[:, FF + HALF :])
    own = jnp.concatenate([both[:, :FF], rest], axis=1)
    return (
        section_out[None, :, :L],
        section_grad[None, :, :L],
        own[None],
        scatter(bias_grad[0])[None],
        scatter(gain_grad[0])[None],
        scatter(shift_grad[0])[None],
    )


def solution(mesh):
    placed = (
        P("dp", None, None),
        P("dp", None, None),
        P("dp"),
        P("dp", None),
        P("section", None, None),
        P("section", None),
        P("section", None),
        P("section", None),
        P(),
    )
    return jax.shard_map(
        shards,
        mesh=mesh,
        in_specs=placed,
        out_specs=(
            P("section", "dp", None, None),
            P("section", "dp", None, None),
            P("section", "dp", None),
            P("section", "dp"),
            P("section", "dp"),
            P("section", "dp"),
        ),
        check_vma=False,
    )
```

time: 1300 us -> 425 us (0.33); the launches traced: 1280 us -> 425 us
  other arithmetic: 314 us -> 17.6 us
  matrix products: 275 us -> 0 us
  local copies, waits for them, and re-layouts: 180 us -> 9.5 us
  Pallas kernels: 0 us -> 163 us
  starting transfers between devices: 123 us -> 2.51 us
  waiting for transfers between devices: 292 us -> 191 us
  loops' own time: 56.5 us -> 0 us
    dot_general x42 -> x0, matrix products: 275 us -> none  [the longest x18 132 us: contract_cols(): lax.dot_general(left, right, (((1,), (1,)), ((), ())), preferred_element_...]
    add x42 -> x0, other arithmetic: 188 us -> none  [the longest x36 183 us: backward_round(): totals = jax.tree.map(jnp.add, totals, tuple(results[1:]))]
    ppermute x18 -> x1, waiting for transfers between devices: 186 us -> 0.01 us  [shards(): arrived = lax.ppermute(both[:, FF:FF + HALF], 'section', pairs)]
    pallas_call x0 -> x1, Pallas kernels: none -> 163 us  [shards(): pl.pallas_call(functools.partial(pipeline_kernel, cfg), out_shape=[jax.Sh...]
    ppermute x18 -> x1, starting transfers between devices: 123 us -> 2.47 us  [shards(): arrived = lax.ppermute(both[:, FF:FF + HALF], 'section', pairs)]
    reduce_scatter x1, waiting for transfers between devices: 106 us -> 191 us  [scatter(): return lax.psum_scatter(value, 'dp', scatter_dimension=0, tiled=True)]
    another operation x26 -> x0, loops' own time: 49.3 us -> none  [the longest x9 25.2 us: backward_round(): lax.cond(active, working, resting_back, (current, grad_output, valid_mask...]
    dynamic_update_slice x26 -> x0, other arithmetic: 43.5 us -> none  [store_slot(): lax.dynamic_update_index_in_dim(buffer, jnp.where(active, value, previous...]
  transfers between devices with their start and end apart: 19 -> 2, of which waited for: 17 -> 1; matrix products, arithmetic and copies ran while one was open for 20% -> 1% of each run, Pallas kernels for 0% -> 0%
where the time goes in v1:
time: 425 us
  waiting for transfers between devices  191 us (45%)
  Pallas kernels  163 us (38%)
  blocking collectives  26 us (6%)
  other arithmetic  17.6 us (4%)
  between operations  15.5 us (4%)
  local copies, waits for them, and re-layouts  9.5 us (2%)
    reduce_scatter x1, waiting for transfers between devices, scatter(): return lax.psum_scatter(value, 'dp', scatter_dimension=0, tiled=True)  191 us
    pallas_call x1, Pallas kernels, shards(): pl.pallas_call(functools.partial(pipeline_kernel, cfg), out_shape=[jax.Sh...  163 us
    unnamed x1, blocking collectives  26 us
    concatenate x1, other arithmetic, shards(): both = scatter(jnp.concatenate([g1, g2], axis=1))  14.5 us
  transfers between devices with their start and end apart: 2, of which 1 were waited for; matrix products, arithmetic and copies ran while one was open for 1% of the time, Pallas kernels for 0%

profile of v1, /device:TPU:2, one launch (start us, length us, event | category | flops | bytes accessed | tf_op | source)
XLA Modules:
  0.0 424.8 jit_solution(6989748662541822163)
XLA Ops:
  7.2 0.0 reduce-scatter.2.cloned.1.call-start
  7.2 0.9 convert_element_type.10
  8.2 0.1 copy.19
  8.2 0.1 mul.25
  8.3 0.1 mul.26
  8.5 0.1 copy.20
  8.6 0.2 mul.23
  8.8 0.3 mul.24
  9.1 0.2 copy.21
  9.2 0.7 broadcast_multiply_fusion.fmap_ref
  9.9 162.9 %pipeline.1 = (bf16[6,208,768]{2,1,0:T(8,128)(2,1)}, bf16[6,208,768]{2,1,0:T(8,128)(2,1)}, f32[768,3072]{1,0:T(8,128)}, f32[768,3072]{1,0:T(8,128)}, f32[1,3072]...) custom-call(s32[6]{0:T(128)} %len_ref.1, bf16[6,202,768]{2,1,0:T(8,128)(2,1)} %x_hbm.1, bf16[6,202,768]{2,1,0:T(8,128)(2,1)} %cot_hbm.1, ...), custom_call_target="tpu_custom_call" | custom-call | tf_op jit(solution)/shard_map/pipeline/pallas_call | solution.py:482
  172.8 14.5 %pad_maximum_fusion = f32[768,6144]{1,0:T(8,128)} fusion(f32[768,3072]{1,0:T(8,128)} %get-tuple-element.16, f32[768,3072]{1,0:T(8,128)} %get-tuple-element.15), kind=kLoop, calls=%fused_computation | loop fusion | flops 4718592 | bytes 37748736 | tf_op jit(solution)/shard_map/concatenate | solution.py:544
  187.4 0.0 copy-start.2
  187.4 0.0 copy-start.1
  187.4 0.0 reduce-scatter.2.cloned.1.call-update
  187.4 190.7 %reduce-scatter.2.cloned.1.call-done = f32[96,6144]{1,0:T(8,128)} async-done(((f32[768,6144]{1,0:T(8,128)}), f32[96,6144]{1,0:T(8,128)}) %reduce-scatter.2.cloned.1.call-update) | async-done | bytes 2359312 | tf_op jit(solution)/shard_map/reduce_scatter | solution.py:542
  378.2 1.1 slice.21
  379.3 2.5 collective-permute-start
  381.8 0.0 copy-done.5
  381.8 0.6 dynamic-slice
  383.7 0.0 copy-done.4
  383.7 0.0 copy-done.3
  383.7 26.0 %all-reduce.3 = (f32[3072]{0:T(1024)S(1)}, f32[768]{0:T(1024)S(1)}, f32[768]{0:T(1024)S(1)}) all-reduce(f32[3072]{0:T(1024)S(1)} %bitcast.18, f32[768]{0:T(1024)S(1)} %reduce, f32[768]{0:T(1024)S(1)} %reduce.1), channel_id=3, replica_groups=mesh['section'=4,'dp'=8] {'dp'}, use_global_device_ids=true, to_apply=%region_1.2.clone | all-reduce | flops 4608 | bytes 36864
  409.7 0.1 dynamic-slice.1
  409.8 0.6 broadcast_in_dim.22
  410.3 0.6 dynamic-slice_bitcast_fusion
  410.9 3.7 slice_bitcast_fusion
  414.6 0.0 collective-permute-done
  414.6 1.7 copy-done
  416.3 0.1 slice_select_fusion
  416.3 0.2 slice-done
  416.6 1.3 maximum_bitcast_fusion
  (10 shorter events, 0.0 us)
Async XLA Ops:
  7.2 371.0 %reduce-scatter.2.cloned.1.call-start = ((), (), s32[]{:S(2)}) async-start(), calls=%async_computation.1 | async-start | bytes 21233664 | tf_op jit(solution)/shard_map/reduce_scatter | solution.py:542
  187.4 194.4 %copy-start.5 = (u32[32]{0:T(128)S(1)}, u32[32]{0:T(128)}, u32[]{:S(2)}) copy-start(u32[32]{0:T(128)} %constant.29) | copy-start | bytes 388
  187.4 196.3 %copy-start.4 = (f32[1,768]{1,0:T(1,128)S(1)}, f32[1,768]{1,0:T(1,128)}, u32[]{:S(2)}) copy-start(f32[1,768]{1,0:T(1,128)} %get-tuple-element.18) | copy-start | bytes 9220
  187.4 196.3 %copy-start.3 = (f32[1,768]{1,0:T(1,128)S(1)}, f32[1,768]{1,0:T(1,128)}, u32[]{:S(2)}) copy-start(f32[1,768]{1,0:T(1,128)} %get-tuple-element.19) | copy-start | bytes 9220
  187.4 196.3 %copy-start.2 = (f32[1,3072]{1,0:T(1,128)S(1)}, f32[1,3072]{1,0:T(1,128)}, u32[]{:S(2)}) copy-start(f32[1,3072]{1,0:T(1,128)} %get-tuple-element.17) | copy-start | bytes 36868
  187.4 223.5 %copy-start.1 = (bf16[6,208,768]{2,1,0:T(8,128)(2,1)S(1)}, bf16[6,208,768]{2,1,0:T(8,128)(2,1)}, u32[]{:S(2)}) copy-start(bf16[6,208,768]{2,1,0:T(8,128)(2,1)} %get-tuple-element.13) | copy-start | bytes 5750788
  379.3 35.3 %collective-permute-start = (f32[96,1536]{1,0:T(8,128)S(1)}, f32[96,1536]{1,0:T(8,128)S(1)}, u32[]{:S(2)}, u32[]{:S(2)}) collective-permute-start(f32[96,1536]{1,0:T(8,128)S(1)} %slice.21), channel_id=1, source_target_pairs={{8,0},{24,16},{9,1},{25,17},{10,2},{26,18},{11,3},{27,19},{12,4},{... | collective-permute-start | bytes 1769480 | tf_op jit(solution)/shard_map/ppermute | solution.py:546
  414.6 1.7 copy-start
  414.6 2.0 slice-start
Sparse Core Ops, SparseCore 0:
  187.6 190.5 reduce-scatter.1

commit v2 on v1

--- a/solution.py
+++ b/solution.py
@@ -33,6 +33,365 @@
     r = lax.broadcasted_iota(jnp.int32, (feature_rows, value_cols), 0) // features
     c = lax.broadcasted_iota(jnp.int32, (feature_rows, value_cols), 1) // head_dim
     return r == c
+
+
+def chunk_columns(cfg, odd):
+    D, FF = cfg[3], cfg[4]
+    wide = FF // D
+    first_kind = 1 + (wide - 1) * odd
+    count = wide + wide * odd
+    return first_kind, count
+
+
+def flat(ref, c):
+    return ref[:, :, c].reshape(ref.shape[0] * ref.shape[1], c.size)
+
+
+def plain_gradients(cfg, odd, xin, dbr, buf_a, buf_b, g_hbm, g_sem, stage):
+    D, FF = cfg[3], cfg[4]
+    first_kind, count = chunk_columns(cfg, odd)
+    wide = FF // D
+
+    def column(k):
+        return pl.ds(pl.multiple_of(k * D, D), D)
+
+    def store(k):
+        cp = pltpu.make_async_copy(stage, g_hbm.at[:, column(k)], g_sem.at[0])
+        cp.start()
+        cp.wait()
+
+    def one(k, carry):
+        @pl.when(k < first_kind)
+        def _():
+            src = column(k + (wide - 1) * (1 - odd))
+            stage[...] = dot_rows(flat(dbr, pl.ds(0, D)), flat(buf_a, src))
+            store(k)
+
+        @pl.when(k >= first_kind)
+        def _():
+            stage[...] = dot_rows(flat(xin, pl.ds(0, D)), flat(buf_b, column(k - first_kind)))
+            store(k)
+
+        return carry
+
+    lax.fori_loop(0, count, one, 0)
+
+    @pl.when(odd == 0)
+    def _():
+        stage[...] = jnp.zeros_like(stage)
+
+        def rest(k, carry):
+            store(k)
+            return carry
+
+        lax.fori_loop(wide, 2 * wide, rest, 0)
+
+
+def reduce_gradients(
+    cfg,
+    s,
+    d,
+    odd,
+    w,
+    u,
+    xin,
+    dbr,
+    buf_a,
+    buf_b,
+    g_hbm,
+    small_ref,
+    ready,
+    tx,
+    td,
+    keep,
+    core_out,
+    line_out,
+    line_down,
+    final,
+    small_in,
+    core_send,
+    core_recv,
+    line_send,
+    up_recv,
+    down_recv,
+    final_sem,
+    cross_send,
+    cross_recv,
+    small_send,
+    small_recv,
+):
+    M, L, LP, D, FF, HD, FE, NS, ND, fscale, in_kernel = cfg
+    Z = ND // 2
+    B = D // ND
+    R = Z * B
+    wide = FF // D
+    keeps = keep.shape[0]
+    p = lax.rem(d, 2)
+    z = d // 2
+    sib = d + 1 - 2 * p
+    first_kind, count = chunk_columns(cfg, odd)
+    dma_to = functools.partial(pltpu.make_async_remote_copy, device_id_type=MESH)
+
+    pl.semaphore_signal(ready.at[0], inc=1, device_id=(s, sib), device_id_type=MESH)
+
+    @pl.when(z > 0)
+    def _():
+        pl.semaphore_signal(ready.at[2], inc=1, device_id=(s, d - 2), device_id_type=MESH)
+
+    @pl.when(z < Z - 1)
+    def _():
+        pl.semaphore_signal(ready.at[1], inc=1, device_id=(s, d + 2), device_id_type=MESH)
+
+    def small_copy(o):
+        return dma_to(
+            small_ref,
+            small_in.at[d],
+            small_send.at[o],
+            small_recv.at[d],
+            device_id=(s, lax.rem(d + o, ND)),
+        )
+
+    def small_wait(o):
+        j = lax.rem(d + o, ND)
+        return dma_to(
+            small_ref,
+            small_in.at[j],
+            small_send.at[o],
+            small_recv.at[j],
+            device_id=(s, j),
+        )
+
+    for o in range(1, ND):
+        small_copy(o).start()
+    small_in[d] = small_ref[...]
+
+    for src, dst in ((dbr, td), (xin, tx)):
+        for i in range(D // 256):
+            turned = flat(src, pl.ds(256 * i, 256)).T
+            for q in range(8):
+                t = 8 * i + q
+                block = t * 32 // B
+                at = block // 2 * B + t * 32 - block * B
+                dst[block % 2, pl.ds(at, 32), :] = turned[32 * q : 32 * q + 32]
+
+    def column(k):
+        return pl.ds(pl.multiple_of(k * D, D), D)
+
+    def slot(c, zt):
+        r = pl.multiple_of(lax.rem(c, 2) * R + zt * B, 16)
+        return (pl.ds(r, B), column(c // 2))
+
+    def core_place(c):
+        return (pl.ds(pl.multiple_of(lax.rem(c, 2) * R, 16), R), column(c // 2))
+
+    def core_copy(c):
+        return dma_to(
+            core_out.at[lax.rem(c, 2)],
+            w.at[core_place(c)],
+            core_send.at[lax.rem(c, 2)],
+            core_recv.at[c],
+            device_id=(s, sib),
+        )
+
+    def up_copy(c, zt):
+        return dma_to(
+            line_out.at[lax.rem(c, 2), zt],
+            u.at[slot(c, zt)],
+            line_send.at[lax.rem(c, 2), zt],
+            up_recv.at[c, zt],
+            device_id=(s, d + 2),
+        )
+
+    def down_copy(c, zt):
+        return dma_to(
+            line_out.at[lax.rem(c, 2), zt],
+            line_down.at[c, zt],
+            line_send.at[lax.rem(c, 2), zt],
+            down_recv.at[c, zt],
+            device_id=(s, d - 2),
+        )
+
+    def place(c):
+        own = c - first_kind
+        early = c + 2 + (1 - odd)
+        return column(jnp.where(c < first_kind, early, own))
+
+    def own_copy(c):
+        return pltpu.make_async_copy(
+            final.at[lax.rem(c, 2)], g_hbm.at[:, place(c)], final_sem.at[lax.rem(c, 2)]
+        )
+
+    def cross_copy(c):
+        return dma_to(
+            final.at[lax.rem(c, 2)],
+            g_hbm.at[:, column(c + wide)],
+            cross_send.at[lax.rem(c, 2)],
+            cross_recv.at[lax.rem(c, 2)],
+            device_id=(s - 1, d),
+        )
+
+    crossing = 2 * odd
+
+    def final_wait(c):
+        @pl.when((c >= 0) & (c < crossing))
+        def _():
+            cross_copy(c).wait_send()
+
+        @pl.when(c >= crossing)
+        def _():
+            own_copy(c).wait()
+
+    def total(c, zt):
+        return keep[lax.rem(c, keeps), pl.ds(zt * B, B), :] + w[slot(c, zt)].astype(f32)
+
+    near = jnp.minimum(z, Z - 1 - z)
+    far = jnp.maximum(z, Z - 1 - z)
+
+    def step(k, carry):
+        @pl.when(k < count)
+        def _():
+            sl = lax.rem(k, 2)
+
+            def products(left, right):
+                @pl.when(k >= 2)
+                def _():
+                    core_copy(k - 2).wait_send()
+
+                core_out[sl] = dot(left[1 - p], right).astype(bf16)
+
+                @pl.when(k == 0)
+                def _():
+                    pl.semaphore_wait(ready.at[0], 1)
+
+                core_copy(k).start()
+                keep[lax.rem(k, keeps)] = dot(left[p], right)
+
+            @pl.when(k < first_kind)
+            def _():
+                products(td, flat(buf_a, column(k + (wide - 1) * (1 - odd))))
+
+            @pl.when(k >= first_kind)
+            def _():
+                products(tx, flat(buf_b, column(k - first_kind)))
+
+        c_near = k - 1 - near
+
+        @pl.when((c_near >= 0) & (c_near < count))
+        def _():
+            core_copy(c_near).wait_recv()
+
+        c_up = k - 1 - z
+
+        @pl.when((c_up >= 0) & (c_up < count) & (z < Z - 1))
+        def _():
+            @pl.when(c_up == 0)
+            def _():
+                pl.semaphore_wait(ready.at[2], 1)
+
+            for zt in range(Z - 1, 0, -1):
+                @pl.when(zt > z)
+                def _():
+                    @pl.when(c_up >= 2)
+                    def _():
+                        up_copy(c_up - 2, zt).wait_send()
+
+                    @pl.when(z > 0)
+                    def _():
+                        up_copy(c_up, zt).wait_recv()
+                        line_out[lax.rem(c_up, 2), zt] = (
+                            total(c_up, zt) + u[slot(c_up, zt)].astype(f32)
+                        ).astype(bf16)
+
+                    @pl.when(z == 0)
+                    def _():
+                        line_out[lax.rem(c_up, 2), zt] = total(c_up, zt).astype(bf16)
+
+                    up_copy(c_up, zt).start()
+
+        c_down = k - 1 - (Z - 1 - z)
+
+        @pl.when((c_down >= 0) & (c_down < count) & (z > 0))
+        def _():
+            @pl.when(c_down == 0)
+            def _():
+                pl.semaphore_wait(ready.at[1], 1)
+
+            for zt in range(Z - 1):
+                @pl.when(zt < z)
+                def _():
+                    @pl.when(c_down >= 2)
+                    def _():
+                        down_copy(c_down - 2, zt).wait_send()
+
+                    @pl.when(z < Z - 1)
+                    def _():
+                        down_copy(c_down, zt).wait_recv()
+                        line_out[lax.rem(c_down, 2), zt] = (
+                            total(c_down, zt) + line_down[c_down, zt].astype(f32)
+                        ).astype(bf16)
+
+                    @pl.when(z == Z - 1)
+                    def _():
+                        line_out[lax.rem(c_down, 2), zt] = total(c_down, zt).astype(bf16)
+
+                    down_copy(c_down, zt).start()
+
+        c_own = k - 1 - far
+
+        @pl.when((c_own >= 0) & (c_own < count))
+        def _():
+            sl = lax.rem(c_own, 2)
+            final_wait(c_own - 2)
+            final[sl] = total(c_own, z)
+
+            @pl.when(z > 0)
+            def _():
+                up_copy(c_own, z).wait_recv()
+                final[sl] += u[slot(c_own, z)].astype(f32)
+
+            @pl.when(z < Z - 1)
+            def _():
+                down_copy(c_own, z).wait_recv()
+                final[sl] += line_down[c_own, z].astype(f32)
+
+            @pl.when(c_own < crossing)
+            def _():
+                cross_copy(c_own).start()
+
+            @pl.when(c_own >= crossing)
+            def _():
+                own_copy(c_own).start()
+
+        return carry
+
+    lax.fori_loop(0, count + 1 + far, step, 0)
+
+    for back in (2, 1):
+        c = count - back
+        core_copy(c).wait_send()
+        for zt in range(Z):
+            @pl.when(zt > z)
+            def _():
+                up_copy(c, zt).wait_send()
+
+            @pl.when(zt < z)
+            def _():
+                down_copy(c, zt).wait_send()
+
+        own_copy(c).wait()
+
+    @pl.when((odd == 0) & (s < NS - 1))
+    def _():
+        for c in range(2):
+            cross_copy(c).wait_recv()
+
+    for o in range(1, ND):
+        small_wait(o).wait_recv()
+        small_copy(o).wait_send()
+    acc = small_in[0]
+    for j in range(1, ND):
+        acc = acc + small_in[j]
+    small_ref[...] = acc
 
 
 def pipeline_kernel(
@@ -48,11 +407,8 @@
     fmap_ref,
     out_hbm,
     grad_hbm,
-    g1_hbm,
-    g2_hbm,
-    bias_grad_ref,
-    gain_grad_ref,
-    shift_grad_ref,
+    g_hbm,
+    small_ref,
     w,
     u,
     xin,
@@ -64,12 +420,11 @@
     rbuf,
     buf_a,
     buf_b,
-    szbuf,
-    stage,
     land,
+    out_stage,
+    grad_stage,
     load_sem,
     x_sem,
-    cot_sem,
     u_send,
     u_recv,
     f_send,
@@ -79,8 +434,9 @@
     out_sem,
     grad_sem,
     g_sem,
+    *reduce_refs,
 ):
-    M, L, LP, D, FF, HD, FE, NS, ND, fscale = cfg
+    M, L, LP, D, FF, HD, FE, NS, ND, fscale, in_kernel = cfg
     HALF = FF // 2
     GH = 256 // HD
     G = D // 256
@@ -104,8 +460,14 @@
             pl.semaphore_signal(barrier, inc=1, device_id=(ts, td), device_id_type=MESH)
 
     always = s >= 0
-    greet(always, s, sib)
-    greet(always, s, mate)
+    partners = 2
+    if in_kernel:
+        partners = ND - 1
+        for o in range(1, ND):
+            greet(always, s, lax.rem(d + o, ND))
+    else:
+        greet(always, s, sib)
+        greet(always, s, mate)
     greet(s > 0, s - 1, d)
     greet(s < NS - 1, s + 1, d)
 
@@ -117,29 +479,31 @@
 
     @pl.when(first)
     def _():
-        for m in range(M):
+        for m in range(2):
             pltpu.make_async_copy(x_hbm.at[m], land.at[m], x_sem.at[m]).start()
 
     @pl.when(last)
     def _():
-        for m in range(M):
+        for m in range(2):
             pltpu.make_async_copy(cot_hbm.at[m], land.at[m], x_sem.at[m]).start()
 
     @pl.when(is_ff)
     def _():
         u_copy.start()
 
-    bias_grad_ref[...] = jnp.zeros_like(bias_grad_ref)
-    gain_grad_ref[...] = jnp.zeros_like(gain_grad_ref)
-    shift_grad_ref[...] = jnp.zeros_like(shift_grad_ref)
+    small_ref[...] = jnp.zeros_like(small_ref)
+    bias_grad_ref = small_ref.at[:, pl.ds(0, FF)]
+    gain_grad_ref = small_ref.at[:, pl.ds(FF, D)]
+    shift_grad_ref = small_ref.at[:, pl.ds(FF + D, D)]
+    pad_zero = jnp.zeros((LP - L, D), bf16)
 
     @pl.when(first | last)
     def _():
-        pl.semaphore_wait(barrier, 3)
+        pl.semaphore_wait(barrier, partners + 1)
 
     @pl.when((s > 0) & (s < NS - 1))
     def _():
-        pl.semaphore_wait(barrier, 4)
+        pl.semaphore_wait(barrier, partners + 2)
 
     q0 = lax.rem(d, 4)
     q_own = pl.ds(pl.multiple_of(q0 * quarter, quarter), quarter)
@@ -189,6 +553,13 @@
     head_mask = block_mask(GF, 256, FE, HD)
     pair_mask = jnp.concatenate([head_mask, head_mask], axis=1)
     ones_cols = jnp.ones((LP, 256), bf16)
+
+
+    def sz_at(m, g):
+        slot = m * G + g
+        r = pl.multiple_of(lax.rem(slot, D // GF) * GF, GF)
+        c = pl.multiple_of(slot // (D // GF) * 512, 512)
+        return (pl.ds(r, GF), pl.ds(c, 512))
 
     def norm_forward(m, pre):
         mean = jnp.mean(pre, axis=-1, keepdims=True)
@@ -228,7 +599,7 @@
             buf_a[m, :, pl.ds(D + GF * (G + g), GF)] = fk
             sz = dot_rows(fk, jnp.concatenate([qkv[2], ones_cols], axis=1))
             sz = jnp.where(pair_mask, sz, 0.0).astype(bf16)
-            szbuf[m, g] = sz
+            u[sz_at(m, g)] = sz
             nd = dot(fq, sz)
             buf_a[m, :, pl.ds(3 * D + 256 * g, 256)] = (nd[:, :256] / nd[:, 256:]).astype(bf16)
         branch = dot_cols(buf_a[m, :, pl.ds(3 * D, D)], w[:, pl.ds(3 * D, D)])
@@ -258,7 +629,7 @@
             v = buf_a[m, :, pl.ds(256 * g, 256)]
             fq = buf_a[m, :, pl.ds(D + GF * g, GF)]
             fk = buf_a[m, :, pl.ds(D + GF * (G + g), GF)]
-            sz = szbuf[m, g]
+            sz = u[sz_at(m, g)]
             nd = dot(fq, sz)
             rden = 1.0 / nd[:, 256:]
             dnum = dmix * rden
@@ -312,22 +683,36 @@
         )
 
     def out_copy(m):
-        return pltpu.make_async_copy(out.at[m], out_hbm.at[m], out_sem.at[m])
+        sl = lax.rem(m, 2)
+        return pltpu.make_async_copy(out_stage.at[sl], out_hbm.at[m], out_sem.at[sl])
 
     def grad_copy(m):
-        return pltpu.make_async_copy(dxo.at[m], grad_hbm.at[m], grad_sem.at[m])
-
-    def land_copy(m):
-        return pltpu.make_async_copy(x_hbm.at[m], land.at[m], x_sem.at[m])
-
-    pad_zero = jnp.zeros((LP - L, D), bf16)
+        sl = lax.rem(m, 2)
+        return pltpu.make_async_copy(grad_stage.at[sl], grad_hbm.at[m], grad_sem.at[sl])
+
+    def land_copy(ref, m):
+        sl = lax.rem(m, 2)
+        return pltpu.make_async_copy(ref.at[m], land.at[sl], x_sem.at[sl])
+
+    def write_out(copy, rows, staged, m):
+        @pl.when(m >= 2)
+        def _():
+            copy(m - 2).wait()
+
+        staged[lax.rem(m, 2)] = rows[m, pl.ds(0, L), :]
+        copy(m).start()
+
     eye = lax.broadcasted_iota(jnp.int32, (L, L), 0) == lax.broadcasted_iota(jnp.int32, (L, L), 1)
 
     def forward_step(m):
         @pl.when(first)
         def _():
-            land_copy(m).wait()
-            xin[m] = jnp.concatenate([land[m], pad_zero], axis=0)
+            land_copy(x_hbm, m).wait()
+            xin[m] = jnp.concatenate([land[lax.rem(m, 2)], pad_zero], axis=0)
+
+            @pl.when(m + 2 < M)
+            def _():
+                land_copy(x_hbm, m + 2).start()
 
         @pl.when(s > 0)
         def _():
@@ -345,21 +730,25 @@
         def _():
             next_copy(m).start()
 
-        out_copy(m).start()
+        write_out(out_copy, out, out_stage, m)
 
     def backward_step(m):
         @pl.when(last)
         def _():
-            land_copy(m).wait()
+            land_copy(cot_hbm, m).wait()
             row = jnp.where(
                 lax.broadcasted_iota(jnp.int32, (1, L), 1) < len_ref[m],
                 pred_ref[pl.ds(m, 1), :].astype(f32),
                 0.0,
             )
             col = jnp.sum(jnp.where(eye, row, 0.0), axis=1, keepdims=True)
-            masked = (land[m].astype(f32) * col).astype(bf16)
+            masked = (land[lax.rem(m, 2)].astype(f32) * col).astype(bf16)
             dyin[m] = jnp.concatenate([masked, pad_zero], axis=0)
 
+            @pl.when(m + 2 < M)
+            def _():
+                land_copy(cot_hbm, m + 2).start()
+
         @pl.when(s < NS - 1)
         def _():
             back_copy(m).wait_recv()
@@ -376,7 +765,7 @@
         def _():
             back_copy(m).start()
 
-        grad_copy(m).start()
+        write_out(grad_copy, dxo, grad_stage, m)
 
     back_start = 6 - (s * s) // 3
 
@@ -396,53 +785,23 @@
 
     lax.fori_loop(0, 6 + M, tick, 0)
 
-    def flat(ref, c):
-        return ref[:, :, c].reshape(M * LP, c.size)
-
-    @pl.when(is_ff)
-    def _():
-        for k in range(2):
-            src = (xin, dbr)[k]
-            rhs = (buf_b, buf_a)[k]
-            dst = (g1_hbm, g2_hbm)[k]
-            for j in range(FF // D):
-                c = pl.ds(j * D, D)
-                if j + k > 0:
-                    cp.wait()
-                stage[...] = dot_rows(flat(src, pl.ds(0, D)), flat(rhs, c))
-                cp = pltpu.make_async_copy(stage, dst.at[:, c], g_sem.at[0])
-                cp.start()
-        cp.wait()
-
-    @pl.when(is_attn)
-    def _():
-        for j in range(FF // D):
-            c = pl.ds(j * D, D)
-            if j > 0:
-                cp.wait()
-            if j < 3:
-                stage[...] = dot_rows(flat(xin, pl.ds(0, D)), flat(buf_b, c))
-            else:
-                stage[...] = dot_rows(flat(dbr, pl.ds(0, D)), flat(buf_a, c))
-            cp = pltpu.make_async_copy(stage, g1_hbm.at[:, c], g_sem.at[0])
-            cp.start()
-        cp.wait()
-        stage[...] = jnp.zeros_like(stage)
-        for j in range(FF // D):
-            cp = pltpu.make_async_copy(stage, g2_hbm.at[:, pl.ds(j * D, D)], g_sem.at[0])
-            cp.start()
-            cp.wait()
-
-    @pl.when(is_attn & (s < NS - 1))
-    def _():
-        u_from_section().wait_send()
-
     @pl.when(is_ff)
     def _():
         u_copy_to(q_own, 1, mate).wait_send()
         u_copy_to(q_own, 2, sib).wait_send()
         u_copy_to(q_mate, 3, sib).wait_send()
 
+    if in_kernel:
+        reduce_gradients(
+            cfg, s, d, odd, w, u, xin, dbr, buf_a, buf_b, g_hbm, small_ref, *reduce_refs
+        )
+    else:
+        plain_gradients(cfg, odd, xin, dbr, buf_a, buf_b, g_hbm, g_sem, *reduce_refs)
+
+    @pl.when(is_attn & (s < NS - 1))
+    def _():
+        u_from_section().wait_send()
+
     for m in range(M):
         @pl.when(s < NS - 1)
         def _():
@@ -452,6 +811,7 @@
         def _():
             back_copy(m).wait_send()
 
+    for m in range(M - 2, M):
         out_copy(m).wait()
         grad_copy(m).wait()
 
@@ -472,54 +832,80 @@
     draws = feature_draws.astype(bf16).reshape(G, GH, HD, FE)
     same = jnp.eye(GH, dtype=bf16)
     fmap = (draws[:, :, :, None, :] * same[None, :, None, :, None]).reshape(G, GH * HD, GF)
-    cfg = (M, L, LP, D, FF, HD, FE, NS, ND, fscale)
+    in_kernel = D // ND % 32 == 0
+    cfg = (M, L, LP, D, FF, HD, FE, NS, ND, fscale, in_kernel)
     hbm = pl.BlockSpec(memory_space=pl.ANY)
     vmem = pl.BlockSpec(memory_space=pltpu.VMEM)
     smem = pl.BlockSpec(memory_space=pltpu.SMEM)
     dma = pltpu.SemaphoreType.DMA
     rows_bf = pltpu.VMEM((M, LP, D), bf16)
     wide_bf = pltpu.VMEM((M, LP, FF), bf16)
-    outs = pl.pallas_call(
+    small_size = FF + 2 * D
+    scratch = [
+        pltpu.VMEM((D, FF), bf16),
+        pltpu.VMEM((D, FF), bf16),
+        rows_bf,
+        rows_bf,
+        rows_bf,
+        rows_bf,
+        rows_bf,
+        pltpu.VMEM((M, LP, D), f32),
+        pltpu.VMEM((M, LP, 1), f32),
+        wide_bf,
+        wide_bf,
+        pltpu.VMEM((2, L, D), bf16),
+        pltpu.VMEM((2, L, D), bf16),
+        pltpu.VMEM((2, L, D), bf16),
+        dma((2,)),
+        dma((2,)),
+        dma((4,)),
+        dma((4,)),
+        dma((M,)),
+        dma((M,)),
+        dma((M,)),
+        dma((M,)),
+        dma((2,)),
+        dma((2,)),
+        dma((1,)),
+    ]
+    if in_kernel:
+        Z, B, chunks = ND // 2, D // ND, 2 * FF // D
+        scratch += [
+            pltpu.SemaphoreType.REGULAR((3,)),
+            pltpu.VMEM((2, Z * B, M * LP), bf16),
+            pltpu.VMEM((2, Z * B, M * LP), bf16),
+            pltpu.VMEM((Z + 1, Z * B, D), f32),
+            pltpu.VMEM((2, Z * B, D), bf16),
+            pltpu.VMEM((2, Z, B, D), bf16),
+            pltpu.VMEM((chunks, Z, B, D), bf16),
+            pltpu.VMEM((2, B, D), f32),
+            pltpu.VMEM((ND, 1, small_size), f32),
+            dma((2,)),
+            dma((chunks,)),
+            dma((2, Z)),
+            dma((chunks, Z)),
+            dma((chunks, Z)),
+            dma((2,)),
+            dma((2,)),
+            dma((2,)),
+            dma((ND,)),
+            dma((ND,)),
+        ]
+        g_shape = (B, FF + FF // 2)
+    else:
+        scratch += [pltpu.VMEM((D, D), f32)]
+        g_shape = (D, 2 * FF)
+    section_out, section_grad, grads, small = pl.pallas_call(
         functools.partial(pipeline_kernel, cfg),
         out_shape=[
-            jax.ShapeDtypeStruct((M, LP, D), bf16),
-            jax.ShapeDtypeStruct((M, LP, D), bf16),
-            jax.ShapeDtypeStruct((D, FF), f32),
-            jax.ShapeDtypeStruct((D, FF), f32),
-            jax.ShapeDtypeStruct((1, FF), f32),
-            jax.ShapeDtypeStruct((1, D), f32),
-            jax.ShapeDtypeStruct((1, D), f32),
+            jax.ShapeDtypeStruct((M, L, D), bf16),
+            jax.ShapeDtypeStruct((M, L, D), bf16),
+            jax.ShapeDtypeStruct(g_shape, f32),
+            jax.ShapeDtypeStruct((1, small_size), f32),
         ],
         in_specs=[smem, hbm, hbm, vmem, hbm, vmem, vmem, vmem, vmem],
-        out_specs=[hbm, hbm, hbm, hbm, vmem, vmem, vmem],
-        scratch_shapes=[
-            pltpu.VMEM((D, FF), bf16),
-            pltpu.VMEM((D, FF), bf16),
-            rows_bf,
-            rows_bf,
-            rows_bf,
-            rows_bf,
-            rows_bf,
-            pltpu.VMEM((M, LP, D), f32),
-            pltpu.VMEM((M, LP, 1), f32),
-            wide_bf,
-            wide_bf,
-            pltpu.VMEM((M, G, GF, 512), bf16),
-            pltpu.VMEM((D, D), f32),
-            pltpu.VMEM((M, L, D), bf16),
-            dma((2,)),
-            dma((M,)),
-            dma((M,)),
-            dma((4,)),
-            dma((4,)),
-            dma((M,)),
-            dma((M,)),
-            dma((M,)),
-            dma((M,)),
-            dma((M,)),
-            dma((M,)),
-            dma((1,)),
-        ],
+        out_specs=[hbm, hbm, hbm, vmem],
+        scratch_shapes=scratch,
         compiler_params=pltpu.CompilerParams(
             collective_id=0, has_side_effects=True, vmem_limit_bytes=60 * 2**20
         ),
@@ -535,25 +921,35 @@
         norm_bias,
         fmap,
     )
-    section_out, section_grad, g1, g2, bias_grad, gain_grad, shift_grad = outs
-    HALF = FF // 2
-
-    def scatter(value):
-        return lax.psum_scatter(value, "dp", scatter_dimension=0, tiled=True)
-
-    both = scatter(jnp.concatenate([g1, g2], axis=1))
-    pairs = [(i, i - 1) for i in range(1, NS, 2)]
-    arrived = lax.ppermute(both[:, FF : FF + HALF], "section", pairs)
-    is_attention = lax.axis_index("section") % 2 == 0
-    rest = jnp.where(is_attention, arrived, both[:, FF + HALF :])
-    own = jnp.concatenate([both[:, :FF], rest], axis=1)
+    parts = [small[0, :FF], small[0, FF : FF + D], small[0, FF + D :]]
+    if in_kernel:
+        own = grads
+        d = lax.axis_index("dp")
+        parts = [lax.dynamic_slice_in_dim(v, d * (v.size // ND), v.size // ND) for v in parts]
+    else:
+        def scatter(value):
+            return lax.psum_scatter(value, "dp", scatter_dimension=0, tiled=True)
+
+        HALF = FF // 2
+        both = scatter(grads)
+        parts = [scatter(v) for v in parts]
+        is_attention = lax.axis_index("section") % 2 == 0
+        turned = jnp.where(
+            is_attention,
+            jnp.concatenate([both[:, D:FF], both[:, :D], both[:, FF:]], axis=1),
+            jnp.concatenate([both[:, FF:], both[:, :FF]], axis=1),
+        )
+        pairs = [(i, i - 1) for i in range(1, NS, 2)]
+        arrived = lax.ppermute(turned[:, FF : FF + HALF], "section", pairs)
+        rest = jnp.where(is_attention, arrived, turned[:, FF + HALF :])
+        own = jnp.concatenate([turned[:, :FF], rest], axis=1)
     return (
-        section_out[None, :, :L],
-        section_grad[None, :, :L],
+        section_out[None],
+        section_grad[None],
         own[None],
-        scatter(bias_grad[0])[None],
-        scatter(gain_grad[0])[None],
-        scatter(shift_grad[0])[None],
+        parts[0][None],
+        parts[1][None],
+        parts[2][None],
     )
 
 

time: 425 us -> 240 us (0.56)
  waiting for transfers between devices: 191 us -> 0 us
  Pallas kernels: 163 us -> 226 us
  blocking collectives: 26 us -> 0 us
  other arithmetic: 17.6 us -> 1.65 us
  between operations: 15.5 us -> 0.7 us
    reduce_scatter x1 -> x0, waiting for transfers between devices: 191 us -> none  [scatter(): return lax.psum_scatter(value, 'dp', scatter_dimension=0, tiled=True)]
    pallas_call x1, Pallas kernels: 163 us -> 226 us  [shards(): pl.pallas_call(functools.partial(pipeline_kernel, cfg), out_shape=[jax.Sh...]
    unnamed x1 -> x0, blocking collectives: 26 us -> none
    concatenate x1 -> x0, other arithmetic: 14.5 us -> none  [shards(): both = scatter(jnp.concatenate([g1, g2], axis=1))]
    broadcast_in_dim x3 -> x0, local copies, waits for them, and re-layouts: 4.81 us -> none  [the longest x1 3.66 us: shards(): section_grad[None, :, :L]]
  transfers between devices with their start and end apart: 2 -> 0, of which waited for: 1 -> 0; matrix products, arithmetic and copies ran while one was open for 1% -> 0% of each run, Pallas kernels for 0% -> 0%
where the time goes in v2:
time: 240 us; the launch traced here: 238 us
  Pallas kernels  226 us (94%)
  local copies, waits for them, and re-layouts  9.97 us (4%)
    pallas_call x1, Pallas kernels, shards(): pl.pallas_call(functools.partial(pipeline_kernel, cfg), out_shape=[jax.Sh...  226 us
    unnamed x7, local copies, waits for them, and re-layouts  6.42 us

profile of v2, /device:TPU:2, one launch (start us, length us, event | category | flops | bytes accessed | tf_op | source)
XLA Modules:
  0.0 238.5 jit_solution(3959170456085428536)
XLA Ops:
  0.6 0.9 convert_element_type.10
  1.6 0.1 copy.16
  1.6 0.1 mul.30
  1.8 0.3 mul.31
  2.1 0.2 copy.18
  2.3 0.1 mul.32
  2.4 0.1 mul.33
  2.5 0.1 copy.17
  2.6 0.7 broadcast_multiply_fusion.fmap_ref
  3.3 226.1 %pipeline.1 = (bf16[6,202,768]{2,1,0:T(8,128)(2,1)}, bf16[6,202,768]{2,1,0:T(8,128)(2,1)}, f32[96,4608]{1,0:T(8,128)}, f32[1,4608]{1,0:T(1,128)}) custom-call(s32[6]{0:T(128)} %len_ref.1, bf16[6,202,768]{2,1,0:T(8,128)(2,1)} %x_hbm.1, bf16[6,202,768]{2,1,0:T(8,128)(2,1)} %cot_hbm.1, s32[6,202]{1,0:T(8,128)} %pred_ref.1, bf16[1,768,4608]{2,1,0:T(8,128)(2,1)} %slab_hbm.1, ...), custom_call_target="tpu_custom_call" | custom-call | tf_op jit(solution)/shard_map/pipeline/pallas_call | solution.py:898
  229.5 0.7 fusion.1
  230.2 0.6 constant_dynamic-slice_fusion
  230.7 0.7 slice.9
  231.5 0.6 constant_dynamic-slice_fusion.2
  232.0 0.0 copy-start
  232.0 3.0 %copy.22 = bf16[1,6,202,768]{3,2,1,0:T(8,128)(2,1)} copy(bf16[1,6,202,768]{3,2,1,0:T(8,128)(2,1)} %bitcast.9) | data formatting | bytes 3723264
  235.1 0.0 copy-done
  235.1 0.0 copy-start.1
  235.1 1.3 copy.23
  236.3 0.9 copy-done.1
  237.2 1.2 copy.24
  (1 shorter events, 0.0 us)
Async XLA Ops:
  232.0 3.0 %copy-start = (bf16[6,202,768]{2,1,0:T(8,128)(2,1)S(1)}, bf16[6,202,768]{2,1,0:T(8,128)(2,1)}, u32[]{:S(2)}) copy-start(bf16[6,202,768]{2,1,0:T(8,128)(2,1)} %get-tuple-element.11) | copy-start | bytes 5584900
  235.1 2.2 copy-start.1
